TPU v7x, 256 devices: a whole 4x4x8 slice. The times are simulated.
256 devices in a mesh: stack: 4 (over y), plane: 32 (over z, x), phys: 2 (over core).
Axes of the slice: x: 4, y: 4, z: 8, core: 2. Of those that a mesh axis runs over, the one named last changes fastest.
Arguments:
- thermal_offset: float32 [256, 512, 512], P('stack', 'plane', 'phys'), may hold values from -6 to 6
- volume_power_source: float32 [256, 512, 512], P('stack', 'plane', 'phys'), may hold values from -0.024 to 0.024
- substance_code: int32 [256, 512, 512], P('stack', 'plane', 'phys'), may hold values from 0 to 4
- creeping_joint_flag: int32 [256, 512, 512], P('stack', 'plane', 'phys'), may hold values 0 or 1
- imposed_overall_distortion: float32 [256, 512, 512], P('stack', 'plane', 'phys'), may hold values from -1 to 1
- plastic_distortion: float32 [256, 512, 512], P('stack', 'plane', 'phys'), may hold values from -3 to 3
- anand_hardness: float32 [256, 512, 512], P('stack', 'plane', 'phys'), may hold values from 0.8 to 2.4
Outputs:
- new_temperature: float32 [256, 512, 512], P('stack', 'plane', 'phys')
- new_creep_strain: float32 [256, 512, 512], P('stack', 'plane', 'phys')
- new_resistance: float32 [256, 512, 512], P('stack', 'plane', 'phys')
- stress_residual: float32 [256, 512, 512], P('stack', 'plane', 'phys')
Inputs may be any that keep to these rules, and one draw needn't show every extreme that they name: `substance_code`: material of each cell: 0 die, 1 underfill, 2 solder ball, 3 substrate, 4 board.
All inputs are finite; a program needn't handle non-finite values. No bound on the sum of `creeping_joint_flag` on one device may be relied on, other than what follows from the above.
Results may differ from a plain program's by a relative error of at most 0.0003.
Values sent between devices are 32-bit elements; how exact they have to be, the bound alone decides.
A program may use at most 128 MiB of HBM per device.

v0:
```python
import functools

import jax
import jax.numpy as jnp
from jax import lax
from jax.experimental import pallas as pl
from jax.experimental.pallas import tpu as pltpu
from jax.sharding import PartitionSpec as P

MESH = pl.DeviceIdType.MESH
TSTEPS = 3
L, X, W = 64, 16, 128
HALF = L // 2

k_table = (4.0, 0.6, 2.5, 1.2, 0.8)
cap_table = (1.6, 1.8, 1.7, 2.0, 1.9)
mod_table = (1.5, 0.6, 0.9, 1.2, 0.8)
expand_table = (0.1, 0.3, 0.25, 0.15, 0.2)
half_resistance = tuple(0.5 / k for k in k_table)
capacities = tuple(0.0003 * c for c in cap_table)
LAT = 1.2e-05
H_CONV = 0.05
LOG2E = 1.4426950408889634
HALF_LN2 = 0.34657359027997264
RATE = 0.05 * 0.22313016014842982

M_START, M_RZ, M_S, M_UV, M_A, M_B, M_C, M_F = 0, 3, 4, 7, 10, 19, 25, 31
N_MSG = 36


def rcp(x):
    return pl.reciprocal(x)


def lookup(c, t):
    low = jnp.where(c < 1, jnp.float32(t[0]), jnp.float32(t[1]))
    top = jnp.where(c < 4, jnp.float32(t[3]), jnp.float32(t[4]))
    return jnp.where(c < 2, low, jnp.where(c < 3, jnp.float32(t[2]), top))


def flat(ref):
    return ref.reshape(2, (L + 2) * X, W)


def shifted(ref, h, l, off):
    return flat(ref)[h, pl.ds(l * X + X + off, X), :]


def loop(n, body, carry, unroll):
    return lax.fori_loop(0, n, body, carry, unroll=unroll)


def kernel(
    t_in, src_in, code_in, flag_in, imp_in, cre_in, har_in,
    t_out, c_out, h_out, s_out,
    code, flag, temp, src, imp, cre, har,
    rk, cap, ip, el, us, vs, gxm, gxp, gym, gyp, c0, rhs, base, md, ex, fl, stress,
    mid, red, planes, abuf, qbuf,
    sx, sy, xs, ys, rz, uvx, uvy, uvxr, uvyr, bx, by, bxr, byr, qx, qy,
    ghost, ghosty, fx, fy, fxr, fyr, zm, zp,
    in_sem, out_sem, ss, rs,
):
    k = lax.axis_index("stack")
    p = lax.axis_index("plane")
    f = lax.axis_index("phys")
    ns, np_ = 4, 32
    up = {"plane": lax.rem(p + 1, np_)}
    down = {"plane": lax.rem(p + np_ - 1, np_)}
    mate = {"phys": 1 - f}
    others = [{"stack": lax.rem(k + o, ns)} for o in (1, 2, 3)]
    first_col, last_col = f == 0, f == 1

    def dev(where):
        return (where.get("stack", k), where.get("plane", p), where.get("phys", f))

    barrier = pltpu.get_barrier_semaphore()
    peers = [up, down, mate] + others
    for w in peers:
        pl.semaphore_signal(barrier, inc=1, device_id=dev(w), device_id_type=MESH)

    loads = {}
    for i, (name, hbm, vm, off) in enumerate((
        ("code", code_in, code, 0), ("temp", t_in, temp, 1), ("src", src_in, src, 0),
        ("flag", flag_in, flag, 0), ("imp", imp_in, imp, 0), ("cre", cre_in, cre, 0),
        ("har", har_in, har, 0),
    )):
        loads[name] = []
        for h in (0, 1):
            cp = pltpu.make_async_copy(
                hbm.at[:, :, pl.ds(W * h, W)], vm.at[h, pl.ds(off, L)], in_sem.at[i, h]
            )
            cp.start()
            loads[name].append(cp)

    def loaded(name):
        for cp in loads[name]:
            cp.wait()

    def message(i, s, d, where):
        return pltpu.make_async_remote_copy(
            src_ref=s, dst_ref=d, send_sem=ss.at[i], recv_sem=rs.at[i],
            device_id=dev(where), device_id_type=MESH,
        )

    sent = []

    def send(i, s, d, where):
        m = message(i, s, d, where)
        m.start()
        sent.append(m)
        return m

    row = lax.broadcasted_iota(jnp.int32, (X, W), 0)
    lane = lax.broadcasted_iota(jnp.int32, (X, W), 1)
    zero = jnp.float32(0.0)

    loaded("code")

    def tables(i, _):
        for h in (0, 1):
            c = code[h, pl.ds(i * 2, 2)]
            rk[h, pl.ds(i * 2 + 1, 2)] = lookup(c, half_resistance)
            cap[h, pl.ds(i * 2, 2)] = lookup(c, capacities)
        return 0

    loop(L // 2, tables, 0, 4)

    def pack_rows(ref, dst, side, off):
        r = 0 if side == 0 else X - 1
        n = ref.shape[1]
        view = ref.reshape(2, n * X, W)
        for h in (0, 1):
            dst[h] = view[h, pl.ds(off * X + r, L, stride=X), :]

    def pack_column(ref, off, dst):
        def body(l, acc):
            v = pltpu.roll(ref[1 - f, l + off], lax.rem(l + 1 - f, W), axis=1)
            return jnp.where(lane == l, v, acc)

        dst[...] = loop(L, body, jnp.zeros((X, W), jnp.float32), 8)

    loaded("temp")
    for side in (0, 1):
        pack_rows(rk, sx.at[side, 0], side, 1)
        pack_rows(temp, sx.at[side, 1], side, 1)
    pack_column(rk, 1, sy.at[0])
    pack_column(temp, 1, sy.at[1])
    pl.semaphore_wait(barrier, len(peers))
    start = [
        send(M_START, sx.at[1], xs.at[0], up),
        send(M_START + 1, sx.at[0], xs.at[1], down),
        send(M_START + 2, sy, ys, mate),
    ]
    to_below = send(M_RZ, rk.at[:, L], rz, others[0])

    one = jnp.ones((2, X, W), jnp.float32)
    top_cap = cap[:, 0] + jnp.where(k == 0, jnp.float32(H_CONV), zero)
    bottom_cap = cap[:, L - 1] + jnp.where(k == ns - 1, jnp.float32(H_CONV), zero)

    def eliminate(i, carry):
        dt, nt, wt, db, nb, wb = carry
        m = L - 1 - i
        g = rcp(rk[:, i + 1] + rk[:, i + 2])
        dn = g * dt + nt
        nn = cap[:, i + 1] * dn + g * nt
        ipv = dt * rcp(dn)
        e = g * ipv
        ip[:, i] = ipv
        el[:, i] = e
        us[:, i] = ipv * wt
        gb = rcp(rk[:, m + 1] + rk[:, m])
        dbn = gb * db + nb
        nbn = cap[:, m - 1] * dbn + gb * nb
        ipb = db * rcp(dbn)
        eb = gb * ipb
        ip[:, m] = ipb
        el[:, m] = eb
        vs[:, m] = ipb * wb
        return dn, nn, e * wt, dbn, nbn, eb * wb

    dt, nt, wt, db, nb, wb = loop(
        HALF - 1, eliminate, (one, top_cap, one, one, bottom_cap, one), 4
    )
    st, sb = nt * rcp(dt), nb * rcp(db)
    gm = rcp(rk[:, HALF] + rk[:, HALF + 1])
    idet = rcp(st * sb + gm * (st + sb))
    m11, m12, m22 = (sb + gm) * idet, gm * idet, (st + gm) * idet
    mid[0], mid[1], mid[2] = m11, m12, m22
    ut, ub, vt, vb = m11 * wt, m12 * wt, m12 * wb, m22 * wb
    us[:, HALF - 1], us[:, HALF], vs[:, HALF - 1], vs[:, HALF] = ut, ub, vt, vb

    def spikes(i, carry):
        ut, ub, vt, vb = carry
        l, m = HALF - 2 - i, HALF + 1 + i
        e, eb = el[:, l], el[:, m]
        ut = us[:, l] + e * ut
        vt = e * vt
        ub = eb * ub
        vb = vs[:, m] + eb * vb
        us[:, l], vs[:, l], us[:, m], vs[:, m] = ut, vt, ub, vb
        return ut, ub, vt, vb

    ut, ub, vt, vb = loop(HALF - 1, spikes, (ut, ub, vt, vb), 4)
    to_below.wait_recv()
    planes[k, 0] = ut + rz[...] + rk[:, 1]
    planes[k, 1] = vb
    planes[k, 2] = ub
    spread = [
        send(M_S + o, planes.at[k], planes.at[k], others[o]) for o in range(3)
    ]

    def halo_rows(xm, xp, h, l):
        return xm[h, pl.ds(l, 1), :], xp[h, pl.ds(l, 1), :]

    def x_shifts(ref, xm, xp, h, l):
        hm, hp = halo_rows(xm, xp, h, l)
        return (
            jnp.where(row == 0, hm, shifted(ref, h, l, -1)),
            jnp.where(row == X - 1, hp, shifted(ref, h, l, 1)),
        )

    def column_of(hy, l):
        v = pltpu.roll(hy[...], lax.rem(W - l, W), axis=1)
        return jnp.broadcast_to(v[:, 0:1], (X, W))

    def y_shifts(v0, v1, e0, e1):
        r0, r1 = pltpu.roll(v0, 1, axis=1), pltpu.roll(v1, 1, axis=1)
        q0, q1 = pltpu.roll(v0, W - 1, axis=1), pltpu.roll(v1, W - 1, axis=1)
        return (
            (jnp.where(lane == 0, e0, r0), jnp.where(lane == W - 1, q1, q0)),
            (jnp.where(lane == 0, r0, r1), jnp.where(lane == W - 1, e1, q1)),
        )

    for m in start:
        m.wait_recv()
    lat = jnp.float32(LAT)
    sxm = jnp.where((row == 0) & (p == 0), zero, lat)
    sxp = jnp.where((row == X - 1) & (p == np_ - 1), zero, lat)
    sym = (jnp.where((lane == 0) & first_col, zero, lat), lat)
    syp = (lat, jnp.where((lane == W - 1) & last_col, zero, lat))

    def lateral(l, _):
        hy = column_of(ys.at[0], l)
        kc = (rk[0, l + 1], rk[1, l + 1])
        ysh = y_shifts(kc[0], kc[1], hy, hy)
        for h in (0, 1):
            km, kp = x_shifts(rk, xs.at[0, 0], xs.at[1, 0], h, l)
            a = sxm * rcp(kc[h] + km)
            b = sxp * rcp(kc[h] + kp)
            c = sym[h] * rcp(kc[h] + ysh[h][0])
            d = syp[h] * rcp(kc[h] + ysh[h][1])
            gxm[h, l], gxp[h, l], gym[h, l], gyp[h, l] = a, b, c, d
            c0[h, l] = cap[h, l] - ((a + b) + (c + d))
        return 0

    loop(L, lateral, 0, 2)

    for side in (0, 1):
        pack_rows(us, uvx.at[side, 0], side, 0)
        pack_rows(vs, uvx.at[side, 1], side, 0)
    pack_column(us, 0, uvy.at[0])
    pack_column(vs, 0, uvy.at[1])
    uv = [
        send(M_UV, uvx.at[1], uvxr.at[0], up),
        send(M_UV + 1, uvx.at[0], uvxr.at[1], down),
        send(M_UV + 2, uvy, uvyr, mate),
    ]

    def right_side(xm, xp, hy_ref):
        def body(l, carry):
            bf, bl = carry
            hy = column_of(hy_ref, l)
            tc = (temp[0, l + 1], temp[1, l + 1])
            ysh = y_shifts(tc[0], tc[1], hy, hy)
            nf, nl = [], []
            for h in (0, 1):
                tm, tp = x_shifts(temp, xm, xp, h, l)
                d = (c0[h, l] * tc[h] + src[h, l]) + (
                    (gxm[h, l] * tm + gxp[h, l] * tp)
                    + (gym[h, l] * ysh[h][0] + gyp[h, l] * ysh[h][1])
                )
                rhs[h, l] = d
                nf.append(bf[h] + us[h, l] * d)
                nl.append(bl[h] + vs[h, l] * d)
            return tuple(nf), tuple(nl)

        z = jnp.zeros((X, W), jnp.float32)
        return loop(L, body, ((z, z), (z, z)), 2)

    def block_solve():
        def forward(i, carry):
            t, b = carry
            m = L - 1 - i
            base[:, i] = ip[:, i] * t
            base[:, m] = ip[:, m] * b
            return rhs[:, i + 1] + el[:, i] * t, rhs[:, m - 1] + el[:, m] * b

        t, b = loop(HALF - 1, forward, (rhs[:, 0], rhs[:, L - 1]), 4)
        t, b = mid[0] * t + mid[1] * b, mid[1] * t + mid[2] * b
        base[:, HALF - 1], base[:, HALF] = t, b

        def backward(i, carry):
            t, b = carry
            l, m = HALF - 2 - i, HALF + 1 + i
            t = base[:, l] + el[:, l] * t
            b = base[:, m] + el[:, m] * b
            base[:, l], base[:, m] = t, b
            return t, b

        loop(HALF - 1, backward, (t, b), 4)

    def correct(qt, qb):
        def body(i, _):
            temp[:, i + 1] = base[:, i] + (us[:, i] * qt + vs[:, i] * qb)
            return 0

        loop(L, body, 0, 4)

    def creep_tables(i, _):
        for h in (0, 1):
            at = pl.ds(i * 2, 2)
            c = code[h, at]
            md[h, at] = lookup(c, mod_table)
            ex[h, at] = lookup(c, expand_table)
            fl[h, at] = jnp.where(flag[h, at] == 1, jnp.float32(RATE), zero)
        return 0

    def creep(last):
        def body(i, _):
            t = temp[:, i + 1]
            c, hd, m = cre[:, i], har[:, i], md[:, i]
            load = imp[:, i] - ex[:, i] * t
            s = m * (load - c)
            z = jnp.abs(s) * (rcp(hd) * jnp.float32(0.5 * LOG2E))
            d = jnp.exp2(z - 1.0) - jnp.exp2(-1.0 - z)
            arr = jnp.exp2(jnp.float32(0.5 * LOG2E) * jnp.tanh(0.25 * t + jnp.float32(HALF_LN2)))
            rate = (fl[:, i] * arr) * d
            q = jnp.exp2(jnp.float32(-0.1 * LOG2E) * jnp.log(0.5 + d))
            gap = 1.0 - (0.5 * hd) * q
            size = jnp.abs(gap)
            root = size * lax.rsqrt(jnp.maximum(size, jnp.float32(1e-30)))
            har[:, i] = hd + (gap * root) * rate
            cn = c + jnp.where(s < 0.0, -rate, rate)
            cre[:, i] = cn
            if last:
                stress[:, i + 1] = m * (load - cn)
            return 0

        loop(L, body, 0, 4)

    xm, xp, hy_ref = xs.at[0, 1], xs.at[1, 1], ys.at[1]
    loaded("src")
    for n in range(TSTEPS):
        bf, bl = right_side(xm, xp, hy_ref)
        for h in (0, 1):
            abuf[n, k, 0, h] = bf[h]
            abuf[n, k, 1, h] = bl[h]
        ends = [
            send(M_A + 3 * n + o, abuf.at[n, k], abuf.at[n, k], others[o]) for o in range(3)
        ]
        block_solve()
        more = n < TSTEPS - 1
        if more:
            for side in (0, 1):
                pack_rows(base, bx.at[n, side], side, 0)
            pack_column(base, 0, by.at[n])
            bases = [
                send(M_B + 3 * n, bx.at[n, 1], bxr.at[n, 0], up),
                send(M_B + 3 * n + 1, bx.at[n, 0], bxr.at[n, 1], down),
                send(M_B + 3 * n + 2, by.at[n], byr.at[n], mate),
            ]
        if n == 0:
            loaded("flag")
            loop(L // 2, creep_tables, 0, 2)
            for m in spread:
                m.wait_recv()
            a1 = planes[0, 1] + planes[1, 0]
            a2 = planes[1, 1] + planes[2, 0]
            a3 = planes[2, 1] + planes[3, 0]
            b1, b2 = planes[1, 2], planes[2, 2]
            d12 = a1 * a2 - b1 * b1
            idet = rcp(d12 * a3 - a1 * (b2 * b2))
            v11, v12, v13 = (a2 * a3 - b2 * b2) * idet, b1 * a3 * idet, b1 * b2 * idet
            v22, v23, v33 = a1 * a3 * idet, a1 * b2 * idet, d12 * idet
            table = ((v11, v12, v13), (v12, v22, v23), (v13, v23, v33))
            for j in range(3):
                for r, shift, sign in ((0, 0, 1.0), (1, 1, -1.0)):
                    at = k + shift
                    v = jnp.where(
                        at == 1, table[0][j],
                        jnp.where(at == 2, table[1][j], jnp.where(at == 3, table[2][j], zero)),
                    )
                    red[r, j] = v * sign
        else:
            if n == 1:
                for name in ("imp", "cre", "har"):
                    loaded(name)
            creep(False)
        for m in ends:
            m.wait_recv()
        r = [abuf[n, j, 1] - abuf[n, j + 1, 0] for j in range(3)]
        qt, qb = [
            red[s, 0] * r[0] + red[s, 1] * r[1] + red[s, 2] * r[2] for s in (0, 1)
        ]
        if more:
            qbuf[n, 0], qbuf[n, 1] = qt, qb
            fluxes = [
                send(M_C + 3 * n, qbuf.at[n, :, :, pl.ds(8, 8)], qx.at[n, 0], up),
                send(M_C + 3 * n + 1, qbuf.at[n, :, :, pl.ds(0, 8)], qx.at[n, 1], down),
                send(M_C + 3 * n + 2, qbuf.at[n, :, 1 - f], qy.at[n], mate),
            ]
        correct(qt, qb)
        if more:
            if n == 0:
                for m in uv:
                    m.wait_recv()
            for m in bases + fluxes:
                m.wait_recv()
            for side, at in ((0, 7), (1, 0)):
                for h in (0, 1):
                    ghost[side, h] = bxr[n, side, h] + (
                        uvxr[side, 0, h] * qx[n, side, 0, h, at : at + 1, :]
                        + uvxr[side, 1, h] * qx[n, side, 1, h, at : at + 1, :]
                    )
            col = [
                jnp.broadcast_to(pltpu.roll(qy[n, s], f, axis=1)[:, 0:1], (X, W)) for s in (0, 1)
            ]
            ghosty[...] = byr[n] + (uvyr[0] * col[0] + uvyr[1] * col[1])
            xm, xp, hy_ref = ghost.at[0], ghost.at[1], ghosty

    stores = []

    def store(i, vm, off, hbm):
        for h in (0, 1):
            cp = pltpu.make_async_copy(
                vm.at[h, pl.ds(off, L)], hbm.at[:, :, pl.ds(W * h, W)], out_sem.at[i, h]
            )
            cp.start()
            stores.append(cp)

    store(0, temp, 1, t_out)
    creep(True)
    store(1, cre, 0, c_out)
    store(2, har, 0, h_out)

    for side in (0, 1):
        pack_rows(stress, fx.at[side], side, 1)
    pack_column(stress, 1, fy)
    edges = [
        send(M_F, fx.at[1], fxr.at[0], up),
        send(M_F + 1, fx.at[0], fxr.at[1], down),
        send(M_F + 2, fy, fyr, mate),
        send(M_F + 3, stress.at[:, L], zm, others[0]),
        send(M_F + 4, stress.at[:, 1], zp, others[2]),
    ]
    for m in edges:
        m.wait_recv()
    stress[:, 0] = jnp.where(k == 0, zero, zm[...])
    stress[:, L + 1] = jnp.where(k == ns - 1, zero, zp[...])
    ghost[0] = jnp.where(p == 0, zero, fxr[0])
    ghost[1] = jnp.where(p == np_ - 1, zero, fxr[1])

    def residual(l, _):
        hy = column_of(fyr, l)
        sc = (stress[0, l + 1], stress[1, l + 1])
        ysh = y_shifts(
            sc[0], sc[1], jnp.where(first_col, zero, hy), jnp.where(last_col, zero, hy)
        )
        for h in (0, 1):
            sm, sp = x_shifts(stress, ghost.at[0], ghost.at[1], h, l)
            rhs[h, l] = (
                ((stress[h, l + 2] + stress[h, l]) + (sm + sp))
                + (ysh[h][0] + ysh[h][1])
            ) - 6.0 * sc[h]
        return 0

    loop(L, residual, 0, 2)
    store(3, rhs, 0, s_out)
    for m in sent:
        m.wait_send()
    for cp in stores:
        cp.wait()


def per_device(*args):
    f32 = jnp.float32
    block = (2, L, X, W)
    tall = (2, L + 2, X, W)

    def vm(*shape):
        return pltpu.VMEM(shape, f32)

    scratch = [
        pltpu.VMEM(block, jnp.int32), pltpu.VMEM(block, jnp.int32), vm(*tall),
        vm(*block), vm(*block), vm(*block), vm(*block),
        vm(*tall),
        *[vm(*block) for _ in range(15)],
        vm(*tall),
        vm(3, 2, X, W), vm(2, 3, 2, X, W),
        vm(4, 3, 2, X, W), vm(TSTEPS, 4, 2, 2, X, W), vm(2, 2, 2, X, W),
        vm(2, 2, 2, L, W), vm(2, X, W), vm(2, 2, 2, L, W), vm(2, X, W),
        vm(2, X, W),
        vm(2, 2, 2, L, W), vm(2, X, W), vm(2, 2, 2, L, W), vm(2, X, W),
        vm(2, 2, 2, L, W), vm(2, X, W), vm(2, 2, 2, L, W), vm(2, X, W),
        vm(2, 2, 2, 2, 8, W), vm(2, 2, X, W),
        vm(2, 2, L, W), vm(X, W),
        vm(2, 2, L, W), vm(X, W), vm(2, 2, L, W), vm(X, W),
        vm(2, X, W), vm(2, X, W),
        pltpu.SemaphoreType.DMA((7, 2)), pltpu.SemaphoreType.DMA((4, 2)),
        pltpu.SemaphoreType.DMA((N_MSG,)), pltpu.SemaphoreType.DMA((N_MSG,)),
    ]
    shape = args[0].shape
    return pl.pallas_call(
        kernel,
        out_shape=[jax.ShapeDtypeStruct(shape, f32)] * 4,
        in_specs=[pl.BlockSpec(memory_space=pl.ANY)] * 7,
        out_specs=[pl.BlockSpec(memory_space=pl.ANY)] * 4,
        scratch_shapes=scratch,
        compiler_params=pltpu.CompilerParams(
            collective_id=0, has_side_effects=True, vmem_limit_bytes=40 << 20
        ),
        name="thermal_creep_step",
    )(*args)


def solution(mesh):
    spec = P("stack", "plane", "phys")
    return jax.shard_map(
        per_device, mesh=mesh, in_specs=(spec,) * 7, out_specs=(spec,) * 4, check_vma=False
    )
```

profile of v0, /device:TPU:8, one launch (start us, length us, event | category | flops | bytes accessed | tf_op | source)
XLA Modules:
  0.0 83.1 jit_solution(4990123735993396147)
XLA Ops:
  0.6 0.0 copy-start
  0.6 1.2 %copy-done = f32[64,16,256]{2,1,0:T(8,128)S(1)} copy-done((f32[64,16,256]{2,1,0:T(8,128)S(1)}, f32[64,16,256]{2,1,0:T(8,128)}, u32[]{:S(2)}) %copy-start) | copy-done | bytes 1048600
  1.9 0.0 copy-start.1
  1.9 1.2 %copy-done.1 = f32[64,16,256]{2,1,0:T(8,128)S(1)} copy-done((f32[64,16,256]{2,1,0:T(8,128)S(1)}, f32[64,16,256]{2,1,0:T(8,128)}, u32[]{:S(2)}) %copy-start.1) | copy-done | bytes 1048600
  3.1 0.0 copy-start.2
  3.1 1.2 %copy-done.2 = s32[64,16,256]{2,1,0:T(8,128)S(1)} copy-done((s32[64,16,256]{2,1,0:T(8,128)S(1)}, s32[64,16,256]{2,1,0:T(8,128)}, u32[]{:S(2)}) %copy-start.2) | copy-done | bytes 1048600
  4.3 0.0 copy-start.3
  4.3 1.2 %copy-done.3 = s32[64,16,256]{2,1,0:T(8,128)S(1)} copy-done((s32[64,16,256]{2,1,0:T(8,128)S(1)}, s32[64,16,256]{2,1,0:T(8,128)}, u32[]{:S(2)}) %copy-start.3) | copy-done | bytes 1048600
  5.5 0.0 copy-start.4
  5.5 1.2 %copy-done.4 = f32[64,16,256]{2,1,0:T(8,128)S(1)} copy-done((f32[64,16,256]{2,1,0:T(8,128)S(1)}, f32[64,16,256]{2,1,0:T(8,128)}, u32[]{:S(2)}) %copy-start.4) | copy-done | bytes 1048600
  6.8 0.0 copy-start.5
  6.8 1.2 %copy-done.5 = f32[64,16,256]{2,1,0:T(8,128)S(1)} copy-done((f32[64,16,256]{2,1,0:T(8,128)S(1)}, f32[64,16,256]{2,1,0:T(8,128)}, u32[]{:S(2)}) %copy-start.5) | copy-done | bytes 1048600
  8.0 0.0 copy-start.6
  8.0 1.2 %copy-done.6 = f32[64,16,256]{2,1,0:T(8,128)S(1)} copy-done((f32[64,16,256]{2,1,0:T(8,128)S(1)}, f32[64,16,256]{2,1,0:T(8,128)}, u32[]{:S(2)}) %copy-start.6) | copy-done | bytes 1048600
  9.2 70.0 %thermal_creep_step.1 = (f32[64,16,256]{2,1,0:T(8,128)S(1)}, f32[64,16,256]{2,1,0:T(8,128)S(1)}, f32[64,16,256]{2,1,0:T(8,128)S(1)}, f32[64,16,256]{2,1,0:T(8,128)S(1)}) custom-call(f32[64,16,256]{2,1,0:T(8,128)S(1)} %copy-done, f32[64,16,256]{2,1,0:T(8,128)S(1)} %copy-done.1, s32[64,16,256]{2,1,0:T(8,128)S(1)} %copy-done.2, s32[64,16,256]{2,1,0:T(8,128)S(1)} %copy-done.3, ...), custom_call_target="tpu_custom_call" | custom-call | tf_op jit(solution)/shard_map/thermal_creep_step/pallas_call | solution.py:513
  79.2 1.0 %copy.15 = f32[64,16,256]{2,1,0:T(8,128)} copy(f32[64,16,256]{2,1,0:T(8,128)S(1)} %get-tuple-element.8) | data formatting | bytes 2097152
  80.2 1.0 %copy.16 = f32[64,16,256]{2,1,0:T(8,128)} copy(f32[64,16,256]{2,1,0:T(8,128)S(1)} %get-tuple-element.9) | data formatting | bytes 2097152
  81.1 1.0 %copy.17 = f32[64,16,256]{2,1,0:T(8,128)} copy(f32[64,16,256]{2,1,0:T(8,128)S(1)} %get-tuple-element.10) | data formatting | bytes 2097152
  82.1 1.0 %copy.18 = f32[64,16,256]{2,1,0:T(8,128)} copy(f32[64,16,256]{2,1,0:T(8,128)S(1)} %get-tuple-element.11) | data formatting | bytes 2097152
Async XLA Ops:
  0.6 1.2 %copy-start = (f32[64,16,256]{2,1,0:T(8,128)S(1)}, f32[64,16,256]{2,1,0:T(8,128)}, u32[]{:S(2)}) copy-start(f32[64,16,256]{2,1,0:T(8,128)} %t_in.1) | copy-start | bytes 3145732
  1.9 1.2 %copy-start.1 = (f32[64,16,256]{2,1,0:T(8,128)S(1)}, f32[64,16,256]{2,1,0:T(8,128)}, u32[]{:S(2)}) copy-start(f32[64,16,256]{2,1,0:T(8,128)} %src_in.1) | copy-start | bytes 3145732
  3.1 1.2 %copy-start.2 = (s32[64,16,256]{2,1,0:T(8,128)S(1)}, s32[64,16,256]{2,1,0:T(8,128)}, u32[]{:S(2)}) copy-start(s32[64,16,256]{2,1,0:T(8,128)} %code_in.1) | copy-start | bytes 3145732
  4.3 1.2 %copy-start.3 = (s32[64,16,256]{2,1,0:T(8,128)S(1)}, s32[64,16,256]{2,1,0:T(8,128)}, u32[]{:S(2)}) copy-start(s32[64,16,256]{2,1,0:T(8,128)} %flag_in.1) | copy-start | bytes 3145732
  5.5 1.2 %copy-start.4 = (f32[64,16,256]{2,1,0:T(8,128)S(1)}, f32[64,16,256]{2,1,0:T(8,128)}, u32[]{:S(2)}) copy-start(f32[64,16,256]{2,1,0:T(8,128)} %imp_in.1) | copy-start | bytes 3145732
  6.8 1.2 %copy-start.5 = (f32[64,16,256]{2,1,0:T(8,128)S(1)}, f32[64,16,256]{2,1,0:T(8,128)}, u32[]{:S(2)}) copy-start(f32[64,16,256]{2,1,0:T(8,128)} %cre_in.1) | copy-start | bytes 3145732
  8.0 1.2 %copy-start.6 = (f32[64,16,256]{2,1,0:T(8,128)S(1)}, f32[64,16,256]{2,1,0:T(8,128)}, u32[]{:S(2)}) copy-start(f32[64,16,256]{2,1,0:T(8,128)} %har_in.1) | copy-start | bytes 3145732
where the time goes:
time: 83.4 us; the launch traced here: 83.1 us
  Pallas kernels  70 us (84%)
  local copies, waits for them, and re-layouts  12.4 us (15%)
    pallas_call x1, Pallas kernels, per_device(): pl.pallas_call(kernel, out_shape=[jax.ShapeDtypeStruct(shape, f32)] * 4,...  70 us
    unnamed x18, local copies, waits for them, and re-layouts  12.4 us

commit v1 on v0

--- a/solution.py
+++ b/solution.py
@@ -89,8 +89,14 @@
             cp = pltpu.make_async_copy(
                 hbm.at[:, :, pl.ds(W * h, W)], vm.at[h, pl.ds(off, L)], in_sem.at[i, h]
             )
-            cp.start()
             loads[name].append(cp)
+
+    def load(*names):
+        for name in names:
+            for cp in loads[name]:
+                cp.start()
+
+    load("code", "temp")
 
     def loaded(name):
         for cp in loads[name]:
@@ -115,6 +121,7 @@
     zero = jnp.float32(0.0)
 
     loaded("code")
+    load("src")
 
     def tables(i, _):
         for h in (0, 1):
@@ -137,9 +144,10 @@
             v = pltpu.roll(ref[1 - f, l + off], lax.rem(l + 1 - f, W), axis=1)
             return jnp.where(lane == l, v, acc)
 
-        dst[...] = loop(L, body, jnp.zeros((X, W), jnp.float32), 8)
+        dst[...] = loop(L, body, jnp.zeros((X, W), jnp.float32), L)
 
     loaded("temp")
+    load("flag", "imp", "cre", "har")
     for side in (0, 1):
         pack_rows(rk, sx.at[side, 0], side, 1)
         pack_rows(temp, sx.at[side, 1], side, 1)
@@ -253,7 +261,7 @@
             c0[h, l] = cap[h, l] - ((a + b) + (c + d))
         return 0
 
-    loop(L, lateral, 0, 2)
+    loop(L, lateral, 0, 8)
 
     for side in (0, 1):
         pack_rows(us, uvx.at[side, 0], side, 0)
@@ -285,7 +293,7 @@
             return tuple(nf), tuple(nl)
 
         z = jnp.zeros((X, W), jnp.float32)
-        return loop(L, body, ((z, z), (z, z)), 2)
+        return loop(L, body, ((z, z), (z, z)), 8)
 
     def block_solve():
         def forward(i, carry):
@@ -474,7 +482,7 @@
             ) - 6.0 * sc[h]
         return 0
 
-    loop(L, residual, 0, 2)
+    loop(L, residual, 0, 8)
     store(3, rhs, 0, s_out)
     for m in sent:
         m.wait_send()
@@ -517,7 +525,7 @@
         out_specs=[pl.BlockSpec(memory_space=pl.ANY)] * 4,
         scratch_shapes=scratch,
         compiler_params=pltpu.CompilerParams(
-            collective_id=0, has_side_effects=True, vmem_limit_bytes=40 << 20
+            collective_id=0, has_side_effects=True, vmem_limit_bytes=60 << 20
         ),
         name="thermal_creep_step",
     )(*args)

time: 83.4 us -> 60.6 us (0.73)
  Pallas kernels: 70 us -> 53.2 us
  local copies, waits for them, and re-layouts: 12.4 us -> 6.53 us
    pallas_call x1, Pallas kernels: 70 us -> 53.2 us  [per_device(): pl.pallas_call(kernel, out_shape=[jax.ShapeDtypeStruct(shape, f32)] * 4,...]
    unnamed x18 -> x10, local copies, waits for them, and re-layouts: 12.4 us -> 6.53 us
where the time goes in v1:
time: 60.6 us; the launch traced here: 60.4 us
  Pallas kernels  53.2 us (88%)
  local copies, waits for them, and re-layouts  6.53 us (11%)
  between operations  0.65 us (1%)
    pallas_call x1, Pallas kernels, per_device(): pl.pallas_call(kernel, out_shape=[jax.ShapeDtypeStruct(shape, f32)] * 4,...  53.2 us
    unnamed x10, local copies, waits for them, and re-layouts  6.53 us

profile of v1, /device:TPU:8, one launch (start us, length us, event | category | flops | bytes accessed | tf_op | source)
XLA Modules:
  0.0 60.4 jit_solution(2829955473528313988)
XLA Ops:
  0.6 53.2 %thermal_creep_step.1 = (f32[64,16,256]{2,1,0:T(8,128)}, f32[64,16,256]{2,1,0:T(8,128)}, f32[64,16,256]{2,1,0:T(8,128)}, f32[64,16,256]{2,1,0:T(8,128)}) custom-call(f32[64,16,256]{2,1,0:T(8,128)} %t_in.1, f32[64,16,256]{2,1,0:T(8,128)} %src_in.1, s32[64,16,256]{2,1,0:T(8,128)} %code_in.1, s32[64,16,256]{2,1,0:T(8,128)} %flag_in.1, f32[64,16,256]{2,1,0:T(8,128)} %imp_in.1, ...), custom_call_target="tpu_custom_call" | custom-call | tf_op jit(solution)/shard_map/thermal_creep_step/pallas_call | solution.py:521
  53.8 0.0 copy-start.2
  53.8 2.4 %copy.15 = f32[64,16,256]{2,1,0:T(8,128)} copy(f32[64,16,256]{2,1,0:T(8,128)} %get-tuple-element.8) | data formatting | bytes 2097152
  56.2 0.0 copy-done.2
  56.2 0.0 copy-start.1
  56.2 1.0 %copy.16 = f32[64,16,256]{2,1,0:T(8,128)} copy(f32[64,16,256]{2,1,0:T(8,128)S(1)} %copy-done.2) | data formatting | bytes 2097152
  57.2 0.6 %copy-done.1 = f32[64,16,256]{2,1,0:T(8,128)S(1)} copy-done((f32[64,16,256]{2,1,0:T(8,128)S(1)}, f32[64,16,256]{2,1,0:T(8,128)}, u32[]{:S(2)}) %copy-start.1) | copy-done | bytes 1048600
  57.8 0.0 copy-start
  57.8 1.0 %copy.17 = f32[64,16,256]{2,1,0:T(8,128)} copy(f32[64,16,256]{2,1,0:T(8,128)S(1)} %copy-done.1) | data formatting | bytes 2097152
  58.8 0.6 %copy-done = f32[64,16,256]{2,1,0:T(8,128)S(1)} copy-done((f32[64,16,256]{2,1,0:T(8,128)S(1)}, f32[64,16,256]{2,1,0:T(8,128)}, u32[]{:S(2)}) %copy-start) | copy-done | bytes 1048600
  59.4 1.0 %copy.18 = f32[64,16,256]{2,1,0:T(8,128)} copy(f32[64,16,256]{2,1,0:T(8,128)S(1)} %copy-done) | data formatting | bytes 2097152
Async XLA Ops:
  53.8 2.4 %copy-start.2 = (f32[64,16,256]{2,1,0:T(8,128)S(1)}, f32[64,16,256]{2,1,0:T(8,128)}, u32[]{:S(2)}) copy-start(f32[64,16,256]{2,1,0:T(8,128)} %get-tuple-element.9) | copy-start | bytes 3145732
  56.2 1.6 %copy-start.1 = (f32[64,16,256]{2,1,0:T(8,128)S(1)}, f32[64,16,256]{2,1,0:T(8,128)}, u32[]{:S(2)}) copy-start(f32[64,16,256]{2,1,0:T(8,128)} %get-tuple-element.10) | copy-start | bytes 3145732
  57.8 1.6 %copy-start = (f32[64,16,256]{2,1,0:T(8,128)S(1)}, f32[64,16,256]{2,1,0:T(8,128)}, u32[]{:S(2)}) copy-start(f32[64,16,256]{2,1,0:T(8,128)} %get-tuple-element.11) | copy-start | bytes 3145732

commit v2 on v1

--- a/solution.py
+++ b/solution.py
@@ -52,13 +52,13 @@
 
 def kernel(
     t_in, src_in, code_in, flag_in, imp_in, cre_in, har_in,
-    t_out, c_out, h_out, s_out,
-    code, flag, temp, src, imp, cre, har,
-    rk, cap, ip, el, us, vs, gxm, gxp, gym, gyp, c0, rhs, base, md, ex, fl, stress,
+    t_end, cre, har, rhs,
+    code, flag, temp, src, imp,
+    rk, cap, ip, el, us, vs, gxm, gxp, gym, gyp, c0, base, md, ex, fl, stress,
     mid, red, planes, abuf, qbuf,
     sx, sy, xs, ys, rz, uvx, uvy, uvxr, uvyr, bx, by, bxr, byr, qx, qy,
-    ghost, ghosty, fx, fy, fxr, fyr, zm, zp,
-    in_sem, out_sem, ss, rs,
+    ghost, ghosty, fx, fy, fxr, fyr, zs, zm, zp, gg, dx,
+    in_sem, ss, rs,
 ):
     k = lax.axis_index("stack")
     p = lax.axis_index("plane")
@@ -119,6 +119,10 @@
     row = lax.broadcasted_iota(jnp.int32, (X, W), 0)
     lane = lax.broadcasted_iota(jnp.int32, (X, W), 1)
     zero = jnp.float32(0.0)
+
+    blank = jnp.zeros((2, X, W), jnp.float32)
+    for edge in (0, L + 1):
+        rk[:, edge], temp[:, edge], stress[:, edge] = blank + 1.0, blank, blank
 
     loaded("code")
     load("src")
@@ -217,15 +221,8 @@
         send(M_S + o, planes.at[k], planes.at[k], others[o]) for o in range(3)
     ]
 
-    def halo_rows(xm, xp, h, l):
-        return xm[h, pl.ds(l, 1), :], xp[h, pl.ds(l, 1), :]
-
-    def x_shifts(ref, xm, xp, h, l):
-        hm, hp = halo_rows(xm, xp, h, l)
-        return (
-            jnp.where(row == 0, hm, shifted(ref, h, l, -1)),
-            jnp.where(row == X - 1, hp, shifted(ref, h, l, 1)),
-        )
+    def x_shifts(ref, h, l):
+        return shifted(ref, h, l, -1), shifted(ref, h, l, 1)
 
     def column_of(hy, l):
         v = pltpu.roll(hy[...], lax.rem(W - l, W), axis=1)
@@ -239,11 +236,10 @@
             (jnp.where(lane == 0, r0, r1), jnp.where(lane == W - 1, e1, q1)),
         )
 
-    for m in start:
-        m.wait_recv()
+    start[2].wait_recv()
     lat = jnp.float32(LAT)
-    sxm = jnp.where((row == 0) & (p == 0), zero, lat)
-    sxp = jnp.where((row == X - 1) & (p == np_ - 1), zero, lat)
+    sxm = jnp.where(row == 0, zero, lat)
+    sxp = jnp.where(row == X - 1, zero, lat)
     sym = (jnp.where((lane == 0) & first_col, zero, lat), lat)
     syp = (lat, jnp.where((lane == W - 1) & last_col, zero, lat))
 
@@ -252,7 +248,7 @@
         kc = (rk[0, l + 1], rk[1, l + 1])
         ysh = y_shifts(kc[0], kc[1], hy, hy)
         for h in (0, 1):
-            km, kp = x_shifts(rk, xs.at[0, 0], xs.at[1, 0], h, l)
+            km, kp = x_shifts(rk, h, l)
             a = sxm * rcp(kc[h] + km)
             b = sxp * rcp(kc[h] + kp)
             c = sym[h] * rcp(kc[h] + ysh[h][0])
@@ -274,7 +270,7 @@
         send(M_UV + 2, uvy, uvyr, mate),
     ]
 
-    def right_side(xm, xp, hy_ref):
+    def right_side(hy_ref):
         def body(l, carry):
             bf, bl = carry
             hy = column_of(hy_ref, l)
@@ -282,7 +278,7 @@
             ysh = y_shifts(tc[0], tc[1], hy, hy)
             nf, nl = [], []
             for h in (0, 1):
-                tm, tp = x_shifts(temp, xm, xp, h, l)
+                tm, tp = x_shifts(temp, h, l)
                 d = (c0[h, l] * tc[h] + src[h, l]) + (
                     (gxm[h, l] * tm + gxp[h, l] * tp)
                     + (gym[h, l] * ysh[h][0] + gyp[h, l] * ysh[h][1])
@@ -295,6 +291,31 @@
         z = jnp.zeros((X, W), jnp.float32)
         return loop(L, body, ((z, z), (z, z)), 8)
 
+    def side_row(ref, s, h, off):
+        view = ref.reshape(2, ref.shape[1] * X, W)
+        return view[h, pl.ds(off * X + (0 if s == 0 else X - 1), L, stride=X), :]
+
+    def ghost_terms(ghost_rows, bf, bl):
+        nf, nl = [], []
+        for h in (0, 1):
+            f_sum, l_sum = [], []
+            for s in (0, 1):
+                d = gg[s, h] * (ghost_rows[s, h] - side_row(temp, s, h, 1))
+                dx[s, h] = d
+                f_sum.append(jnp.sum(uvx[s, 0, h] * d, axis=0, keepdims=True))
+                l_sum.append(jnp.sum(uvx[s, 1, h] * d, axis=0, keepdims=True))
+            for out, old, sums in ((nf, bf, f_sum), (nl, bl, l_sum)):
+                add = jnp.where(row == 0, sums[0], jnp.where(row == X - 1, sums[1], zero))
+                out.append(old[h] + add)
+        return nf, nl
+
+    def add_rows(ref, rows_ref):
+        view = ref.reshape(2, L * X, W)
+        for h in (0, 1):
+            for s, r in ((0, 0), (1, X - 1)):
+                at = pl.ds(r, L, stride=X)
+                view[h, at, :] = view[h, at, :] + rows_ref[s, h]
+
     def block_solve():
         def forward(i, carry):
             t, b = carry
@@ -317,9 +338,12 @@
 
         loop(HALF - 1, backward, (t, b), 4)
 
-    def correct(qt, qb):
+    def correct(qt, qb, last):
         def body(i, _):
-            temp[:, i + 1] = base[:, i] + (us[:, i] * qt + vs[:, i] * qb)
+            t = base[:, i] + (us[:, i] * qt + vs[:, i] * qb)
+            temp[:, i + 1] = t
+            if last:
+                t_end[:, i] = t
             return 0
 
         loop(L, body, 0, 4)
@@ -333,39 +357,67 @@
             fl[h, at] = jnp.where(flag[h, at] == 1, jnp.float32(RATE), zero)
         return 0
 
-    def creep(last):
+    def creep_cell(t, c, hd, m, e, im, active):
+        load = im - e * t
+        s = m * (load - c)
+        z = jnp.abs(s) * (rcp(hd) * jnp.float32(0.5 * LOG2E))
+        d = jnp.exp2(z - 1.0) - jnp.exp2(-1.0 - z)
+        arr = jnp.exp2(jnp.float32(0.5 * LOG2E) * jnp.tanh(0.25 * t + jnp.float32(HALF_LN2)))
+        rate = (active * arr) * d
+        q = jnp.exp2(jnp.float32(-0.1 * LOG2E) * jnp.log(0.5 + d))
+        gap = 1.0 - (0.5 * hd) * q
+        size = jnp.abs(gap)
+        root = size * lax.rsqrt(jnp.maximum(size, jnp.float32(1e-30)))
+        cn = c + jnp.where(s < 0.0, -rate, rate)
+        return cn, hd + (gap * root) * rate, m * (load - cn)
+
+    state = (cre, har, md, ex, imp, fl)
+
+    def creep():
         def body(i, _):
-            t = temp[:, i + 1]
-            c, hd, m = cre[:, i], har[:, i], md[:, i]
-            load = imp[:, i] - ex[:, i] * t
-            s = m * (load - c)
-            z = jnp.abs(s) * (rcp(hd) * jnp.float32(0.5 * LOG2E))
-            d = jnp.exp2(z - 1.0) - jnp.exp2(-1.0 - z)
-            arr = jnp.exp2(jnp.float32(0.5 * LOG2E) * jnp.tanh(0.25 * t + jnp.float32(HALF_LN2)))
-            rate = (fl[:, i] * arr) * d
-            q = jnp.exp2(jnp.float32(-0.1 * LOG2E) * jnp.log(0.5 + d))
-            gap = 1.0 - (0.5 * hd) * q
-            size = jnp.abs(gap)
-            root = size * lax.rsqrt(jnp.maximum(size, jnp.float32(1e-30)))
-            har[:, i] = hd + (gap * root) * rate
-            cn = c + jnp.where(s < 0.0, -rate, rate)
-            cre[:, i] = cn
-            if last:
-                stress[:, i + 1] = m * (load - cn)
+            cre[:, i], har[:, i], _s = creep_cell(temp[:, i + 1], *[a[:, i] for a in state])
             return 0
 
         loop(L, body, 0, 4)
 
-    xm, xp, hy_ref = xs.at[0, 1], xs.at[1, 1], ys.at[1]
+    def last_creep(h):
+        def body(i, _):
+            cre[h, i], har[h, i], stress[h, i + 1] = creep_cell(
+                temp[h, i + 1], *[a[h, i] for a in state]
+            )
+            return 0
+
+        loop(L, body, 0, 8)
+
+    hy_ref = ys.at[1]
     loaded("src")
     for n in range(TSTEPS):
-        bf, bl = right_side(xm, xp, hy_ref)
+        bf, bl = right_side(hy_ref)
+        if n == 0:
+            for m in start[:2]:
+                m.wait_recv()
+            for s in (0, 1):
+                wide = jnp.where(p == (0 if s == 0 else np_ - 1), zero, lat)
+                for h in (0, 1):
+                    gg[s, h] = wide * rcp(sx[s, 0, h] + xs[s, 0, h])
+            bf, bl = ghost_terms(xs.at[:, 1], bf, bl)
+        else:
+            for m in bases[:2] + fluxes[:2]:
+                m.wait_recv()
+            for side, at in ((0, 7), (1, 0)):
+                for h in (0, 1):
+                    ghost[side, h] = bxr[n - 1, side, h] + (
+                        uvxr[side, 0, h] * qx[n - 1, side, 0, h, at : at + 1, :]
+                        + uvxr[side, 1, h] * qx[n - 1, side, 1, h, at : at + 1, :]
+                    )
+            bf, bl = ghost_terms(ghost, bf, bl)
         for h in (0, 1):
             abuf[n, k, 0, h] = bf[h]
             abuf[n, k, 1, h] = bl[h]
         ends = [
             send(M_A + 3 * n + o, abuf.at[n, k], abuf.at[n, k], others[o]) for o in range(3)
         ]
+        add_rows(rhs, dx)
         block_solve()
         more = n < TSTEPS - 1
         if more:
@@ -403,7 +455,7 @@
             if n == 1:
                 for name in ("imp", "cre", "har"):
                     loaded(name)
-            creep(False)
+            creep()
         for m in ends:
             m.wait_recv()
         r = [abuf[n, j, 1] - abuf[n, j + 1, 0] for j in range(3)]
@@ -417,56 +469,38 @@
                 send(M_C + 3 * n + 1, qbuf.at[n, :, :, pl.ds(0, 8)], qx.at[n, 1], down),
                 send(M_C + 3 * n + 2, qbuf.at[n, :, 1 - f], qy.at[n], mate),
             ]
-        correct(qt, qb)
+        correct(qt, qb, not more)
         if more:
             if n == 0:
                 for m in uv:
                     m.wait_recv()
-            for m in bases + fluxes:
-                m.wait_recv()
-            for side, at in ((0, 7), (1, 0)):
-                for h in (0, 1):
-                    ghost[side, h] = bxr[n, side, h] + (
-                        uvxr[side, 0, h] * qx[n, side, 0, h, at : at + 1, :]
-                        + uvxr[side, 1, h] * qx[n, side, 1, h, at : at + 1, :]
-                    )
+            bases[2].wait_recv()
+            fluxes[2].wait_recv()
             col = [
                 jnp.broadcast_to(pltpu.roll(qy[n, s], f, axis=1)[:, 0:1], (X, W)) for s in (0, 1)
             ]
             ghosty[...] = byr[n] + (uvyr[0] * col[0] + uvyr[1] * col[1])
-            xm, xp, hy_ref = ghost.at[0], ghost.at[1], ghosty
-
-    stores = []
-
-    def store(i, vm, off, hbm):
-        for h in (0, 1):
-            cp = pltpu.make_async_copy(
-                vm.at[h, pl.ds(off, L)], hbm.at[:, :, pl.ds(W * h, W)], out_sem.at[i, h]
-            )
-            cp.start()
-            stores.append(cp)
-
-    store(0, temp, 1, t_out)
-    creep(True)
-    store(1, cre, 0, c_out)
-    store(2, har, 0, h_out)
-
-    for side in (0, 1):
-        pack_rows(stress, fx.at[side], side, 1)
-    pack_column(stress, 1, fy)
+            hy_ref = ghosty
+
+    for s in (0, 1):
+        for h in (0, 1):
+            fx[s, h] = creep_cell(
+                side_row(temp, s, h, 1), *[side_row(a, s, h, 0) for a in state]
+            )[2]
+    for j, l in ((0, 0), (1, L - 1)):
+        zs[j] = creep_cell(temp[:, l + 1], *[a[:, l] for a in state])[2]
     edges = [
         send(M_F, fx.at[1], fxr.at[0], up),
         send(M_F + 1, fx.at[0], fxr.at[1], down),
-        send(M_F + 2, fy, fyr, mate),
-        send(M_F + 3, stress.at[:, L], zm, others[0]),
-        send(M_F + 4, stress.at[:, 1], zp, others[2]),
+        send(M_F + 3, zs.at[1], zm, others[0]),
+        send(M_F + 4, zs.at[0], zp, others[2]),
     ]
-    for m in edges:
-        m.wait_recv()
-    stress[:, 0] = jnp.where(k == 0, zero, zm[...])
-    stress[:, L + 1] = jnp.where(k == ns - 1, zero, zp[...])
-    ghost[0] = jnp.where(p == 0, zero, fxr[0])
-    ghost[1] = jnp.where(p == np_ - 1, zero, fxr[1])
+    last_creep(1 - f)
+    pack_column(stress, 1, fy)
+    beside = send(M_F + 2, fy, fyr, mate)
+    last_creep(f)
+
+    beside.wait_recv()
 
     def residual(l, _):
         hy = column_of(fyr, l)
@@ -475,7 +509,8 @@
             sc[0], sc[1], jnp.where(first_col, zero, hy), jnp.where(last_col, zero, hy)
         )
         for h in (0, 1):
-            sm, sp = x_shifts(stress, ghost.at[0], ghost.at[1], h, l)
+            sm, sp = x_shifts(stress, h, l)
+            sm, sp = jnp.where(row == 0, zero, sm), jnp.where(row == X - 1, zero, sp)
             rhs[h, l] = (
                 ((stress[h, l + 2] + stress[h, l]) + (sm + sp))
                 + (ysh[h][0] + ysh[h][1])
@@ -483,10 +518,29 @@
         return 0
 
     loop(L, residual, 0, 8)
-    store(3, rhs, 0, s_out)
+    for m in edges:
+        m.wait_recv()
+    rhs[:, 0] = rhs[:, 0] + jnp.where(k == 0, zero, zm[...])
+    rhs[:, L - 1] = rhs[:, L - 1] + jnp.where(k == ns - 1, zero, zp[...])
+    ghost[0] = jnp.where(p == 0, zero, fxr[0])
+    ghost[1] = jnp.where(p == np_ - 1, zero, fxr[1])
+    add_rows(rhs, ghost)
     for m in sent:
         m.wait_send()
-    for cp in stores:
+
+
+def write_out(temp, cre, har, res, t_out, c_out, h_out, s_out, sem):
+    copies = []
+    for i, (vm, hbm) in enumerate(
+        ((temp, t_out), (cre, c_out), (har, h_out), (res, s_out))
+    ):
+        for h in (0, 1):
+            copies.append(pltpu.make_async_copy(
+                vm.at[h], hbm.at[:, :, pl.ds(W * h, W)], sem.at[i, h]
+            ))
+    for cp in copies:
+        cp.start()
+    for cp in copies:
         cp.wait()
 
 
@@ -500,9 +554,9 @@
 
     scratch = [
         pltpu.VMEM(block, jnp.int32), pltpu.VMEM(block, jnp.int32), vm(*tall),
-        vm(*block), vm(*block), vm(*block), vm(*block),
+        vm(*block), vm(*block),
         vm(*tall),
-        *[vm(*block) for _ in range(15)],
+        *[vm(*block) for _ in range(14)],
         vm(*tall),
         vm(3, 2, X, W), vm(2, 3, 2, X, W),
         vm(4, 3, 2, X, W), vm(TSTEPS, 4, 2, 2, X, W), vm(2, 2, 2, X, W),
@@ -513,22 +567,32 @@
         vm(2, 2, 2, 2, 8, W), vm(2, 2, X, W),
         vm(2, 2, L, W), vm(X, W),
         vm(2, 2, L, W), vm(X, W), vm(2, 2, L, W), vm(X, W),
-        vm(2, X, W), vm(2, X, W),
-        pltpu.SemaphoreType.DMA((7, 2)), pltpu.SemaphoreType.DMA((4, 2)),
+        vm(2, 2, X, W), vm(2, X, W), vm(2, X, W),
+        vm(2, 2, L, W), vm(2, 2, L, W),
+        pltpu.SemaphoreType.DMA((7, 2)),
         pltpu.SemaphoreType.DMA((N_MSG,)), pltpu.SemaphoreType.DMA((N_MSG,)),
     ]
     shape = args[0].shape
-    return pl.pallas_call(
+    results = pl.pallas_call(
         kernel,
-        out_shape=[jax.ShapeDtypeStruct(shape, f32)] * 4,
-        in_specs=[pl.BlockSpec(memory_space=pl.ANY)] * 7,
-        out_specs=[pl.BlockSpec(memory_space=pl.ANY)] * 4,
+        out_shape=[jax.ShapeDtypeStruct(s, f32) for s in (block,) * 4],
+        in_specs=[pl.BlockSpec(memory_space=pltpu.HBM)] * 7,
+        out_specs=[pl.BlockSpec(memory_space=pltpu.VMEM)] * 4,
         scratch_shapes=scratch,
         compiler_params=pltpu.CompilerParams(
-            collective_id=0, has_side_effects=True, vmem_limit_bytes=60 << 20
+            collective_id=0, has_side_effects=True, vmem_limit_bytes=49 << 20
         ),
         name="thermal_creep_step",
     )(*args)
+    return pl.pallas_call(
+        write_out,
+        out_shape=[jax.ShapeDtypeStruct(shape, f32)] * 4,
+        in_specs=[pl.BlockSpec(memory_space=pltpu.VMEM)] * 4,
+        out_specs=[pl.BlockSpec(memory_space=pltpu.HBM)] * 4,
+        scratch_shapes=[pltpu.SemaphoreType.DMA((4, 2))],
+        compiler_params=pltpu.CompilerParams(vmem_limit_bytes=16 << 20),
+        name="write_out",
+    )(*results)
 
 
 def solution(mesh):

time: 60.6 us -> 46.4 us (0.77)
  the two profiles are of different devices: /device:TPU:8 before, /device:TPU:1 now
where the time goes in v2:
time: 46.4 us; the launch traced here: 46.3 us
  Pallas kernels  45.6 us (98%)
  between operations  0.64 us (1%)
    pallas_call x1, Pallas kernels, per_device(): pl.pallas_call(kernel, out_shape=[jax.ShapeDtypeStruct(s, f32) for s in (...  43.6 us
    pallas_call x1, Pallas kernels, per_device(): pl.pallas_call(write_out, out_shape=[jax.ShapeDtypeStruct(shape, f32)] *...  2.07 us

profile of v2, /device:TPU:1, one launch (start us, length us, event | category | flops | bytes accessed | tf_op | source)
XLA Modules:
  0.0 46.3 jit_solution(16849293712238741687)
XLA Ops:
  0.6 43.6 %thermal_creep_step.1 = (f32[2,64,16,128]{3,2,1,0:T(8,128)S(1)}, f32[2,64,16,128]{3,2,1,0:T(8,128)S(1)}, f32[2,64,16,128]{3,2,1,0:T(8,128)S(1)}, f32[2,64,16,128]{3,2,1,0:T(8,128)S(1)}) custom-call(f32[64,16,256]{2,1,0:T(8,128)} %t_in.1, f32[64,16,256]{2,1,0:T(8,128)} %src_in.1, s32[64,16,256]{2,1,0:T(8,128)} %code_in.1, s32[64,16,256]{2,1,0:T(8,128)} %flag_in.1, ...), custom_call_target="tpu_custom_call" | custom-call | tf_op jit(solution)/shard_map/thermal_creep_step/pallas_call | solution.py:576
  44.2 2.1 %write_out.1 = (f32[64,16,256]{2,1,0:T(8,128)}, f32[64,16,256]{2,1,0:T(8,128)}, f32[64,16,256]{2,1,0:T(8,128)}, f32[64,16,256]{2,1,0:T(8,128)}) custom-call(f32[2,64,16,128]{3,2,1,0:T(8,128)S(1)} %get-tuple-element.8.temp, f32[2,64,16,128]{3,2,1,0:T(8,128)S(1)} %get-tuple-element.9.cre, f32[2,64,16,128]{3,2,1,0:T(8,128)S(1)} %get-tuple-element.10.har, ...), custom_call_target="tpu_custom_call" | custom-call | tf_op jit(solution)/shard_map/write_out/pallas_call | solution.py:587

commit v3 on v2

--- a/solution.py
+++ b/solution.py
@@ -57,7 +57,7 @@
     rk, cap, ip, el, us, vs, gxm, gxp, gym, gyp, c0, base, md, ex, fl, stress,
     mid, red, planes, abuf, qbuf,
     sx, sy, xs, ys, rz, uvx, uvy, uvxr, uvyr, bx, by, bxr, byr, qx, qy,
-    ghost, ghosty, fx, fy, fxr, fyr, zs, zm, zp, gg, dx,
+    ghost, ghosty, fx, fy, fxr, fyr, zs, zm, zp, gg, dx, pc, qend,
     in_sem, ss, rs,
 ):
     k = lax.axis_index("stack")
@@ -155,15 +155,15 @@
     for side in (0, 1):
         pack_rows(rk, sx.at[side, 0], side, 1)
         pack_rows(temp, sx.at[side, 1], side, 1)
-    pack_column(rk, 1, sy.at[0])
-    pack_column(temp, 1, sy.at[1])
     pl.semaphore_wait(barrier, len(peers))
     start = [
         send(M_START, sx.at[1], xs.at[0], up),
         send(M_START + 1, sx.at[0], xs.at[1], down),
-        send(M_START + 2, sy, ys, mate),
     ]
     to_below = send(M_RZ, rk.at[:, L], rz, others[0])
+    pack_column(rk, 1, sy.at[0])
+    pack_column(temp, 1, sy.at[1])
+    start.append(send(M_START + 2, sy, ys, mate))
 
     one = jnp.ones((2, X, W), jnp.float32)
     top_cap = cap[:, 0] + jnp.where(k == 0, jnp.float32(H_CONV), zero)
@@ -338,12 +338,12 @@
 
         loop(HALF - 1, backward, (t, b), 4)
 
-    def correct(qt, qb, last):
+    def solved(i, qt, qb):
+        return base[:, i] + (us[:, i] * qt + vs[:, i] * qb)
+
+    def correct(qt, qb):
         def body(i, _):
-            t = base[:, i] + (us[:, i] * qt + vs[:, i] * qb)
-            temp[:, i + 1] = t
-            if last:
-                t_end[:, i] = t
+            temp[:, i + 1] = solved(i, qt, qb)
             return 0
 
         loop(L, body, 0, 4)
@@ -379,15 +379,6 @@
             return 0
 
         loop(L, body, 0, 4)
-
-    def last_creep(h):
-        def body(i, _):
-            cre[h, i], har[h, i], stress[h, i + 1] = creep_cell(
-                temp[h, i + 1], *[a[h, i] for a in state]
-            )
-            return 0
-
-        loop(L, body, 0, 8)
 
     hy_ref = ys.at[1]
     loaded("src")
@@ -432,6 +423,9 @@
         if n == 0:
             loaded("flag")
             loop(L // 2, creep_tables, 0, 2)
+            loaded("imp")
+            for j, a in enumerate((md, ex, imp, fl)):
+                pack_column(a, 0, pc.at[2 + j])
             for m in spread:
                 m.wait_recv()
             a1 = planes[0, 1] + planes[1, 0]
@@ -453,9 +447,13 @@
                     red[r, j] = v * sign
         else:
             if n == 1:
-                for name in ("imp", "cre", "har"):
+                for name in ("cre", "har"):
                     loaded(name)
             creep()
+            if not more:
+                pack_column(base, 0, pc.at[6])
+                pack_column(cre, 0, pc.at[0])
+                pack_column(har, 0, pc.at[1])
         for m in ends:
             m.wait_recv()
         r = [abuf[n, j, 1] - abuf[n, j + 1, 0] for j in range(3)]
@@ -469,8 +467,8 @@
                 send(M_C + 3 * n + 1, qbuf.at[n, :, :, pl.ds(0, 8)], qx.at[n, 1], down),
                 send(M_C + 3 * n + 2, qbuf.at[n, :, 1 - f], qy.at[n], mate),
             ]
-        correct(qt, qb, not more)
         if more:
+            correct(qt, qb)
             if n == 0:
                 for m in uv:
                     m.wait_recv()
@@ -482,27 +480,37 @@
             ghosty[...] = byr[n] + (uvyr[0] * col[0] + uvyr[1] * col[1])
             hy_ref = ghosty
 
-    for s in (0, 1):
-        for h in (0, 1):
-            fx[s, h] = creep_cell(
-                side_row(temp, s, h, 1), *[side_row(a, s, h, 0) for a in state]
-            )[2]
+    qend[0], qend[1] = qt, qb
+    col = [
+        jnp.broadcast_to(pltpu.roll(qend[j, 1 - f], 1 - f, axis=1)[:, 0:1], (X, W)) for j in (0, 1)
+    ]
+    tc = pc[6] + (uvy[0] * col[0] + uvy[1] * col[1])
+    used = jnp.where(lane < L, pc[1], jnp.float32(1.0))
+    fy[...] = creep_cell(tc, pc[0], used, *[pc[2 + j] for j in range(4)])[2]
+    beside = send(M_F + 2, fy, fyr, mate)
+    for s, r in ((0, 0), (1, X - 1)):
+        for h in (0, 1):
+            t = side_row(base, s, h, 0) + (
+                uvx[s, 0, h] * qend[0, h, r : r + 1, :] + uvx[s, 1, h] * qend[1, h, r : r + 1, :]
+            )
+            fx[s, h] = creep_cell(t, *[side_row(a, s, h, 0) for a in state])[2]
     for j, l in ((0, 0), (1, L - 1)):
-        zs[j] = creep_cell(temp[:, l + 1], *[a[:, l] for a in state])[2]
+        zs[j] = creep_cell(solved(l, qt, qb), *[a[:, l] for a in state])[2]
     edges = [
         send(M_F, fx.at[1], fxr.at[0], up),
         send(M_F + 1, fx.at[0], fxr.at[1], down),
         send(M_F + 3, zs.at[1], zm, others[0]),
         send(M_F + 4, zs.at[0], zp, others[2]),
     ]
-    last_creep(1 - f)
-    pack_column(stress, 1, fy)
-    beside = send(M_F + 2, fy, fyr, mate)
-    last_creep(f)
-
-    beside.wait_recv()
-
-    def residual(l, _):
+
+    lag = 8
+
+    def last_creep(i):
+        t = solved(i, qt, qb)
+        t_end[:, i] = t
+        cre[:, i], har[:, i], stress[:, i + 1] = creep_cell(t, *[a[:, i] for a in state])
+
+    def residual(l):
         hy = column_of(fyr, l)
         sc = (stress[0, l + 1], stress[1, l + 1])
         ysh = y_shifts(
@@ -515,9 +523,24 @@
                 ((stress[h, l + 2] + stress[h, l]) + (sm + sp))
                 + (ysh[h][0] + ysh[h][1])
             ) - 6.0 * sc[h]
+
+    def first_layers(i, _):
+        last_creep(i)
         return 0
 
-    loop(L, residual, 0, 8)
+    def both(i, _):
+        last_creep(i + lag)
+        residual(i)
+        return 0
+
+    def last_layers(i, _):
+        residual(i + L - lag)
+        return 0
+
+    loop(lag, first_layers, 0, 4)
+    beside.wait_recv()
+    loop(L - lag, both, 0, 4)
+    loop(lag, last_layers, 0, 8)
     for m in edges:
         m.wait_recv()
     rhs[:, 0] = rhs[:, 0] + jnp.where(k == 0, zero, zm[...])
@@ -569,6 +592,7 @@
         vm(2, 2, L, W), vm(X, W), vm(2, 2, L, W), vm(X, W),
         vm(2, 2, X, W), vm(2, X, W), vm(2, X, W),
         vm(2, 2, L, W), vm(2, 2, L, W),
+        vm(7, X, W), vm(2, 2, X, W),
         pltpu.SemaphoreType.DMA((7, 2)),
         pltpu.SemaphoreType.DMA((N_MSG,)), pltpu.SemaphoreType.DMA((N_MSG,)),
     ]

time: 46.4 us -> 45.6 us (0.983)
  the two profiles are of different devices: /device:TPU:1 before, /device:TPU:8 now
where the time goes in v3:
time: 45.6 us; the launch traced here: 44.7 us
  Pallas kernels  44 us (96%)
  between operations  0.64 us (1%)
    pallas_call x1, Pallas kernels, per_device(): pl.pallas_call(kernel, out_shape=[jax.ShapeDtypeStruct(s, f32) for s in (...  41.9 us
    pallas_call x1, Pallas kernels, per_device(): pl.pallas_call(write_out, out_shape=[jax.ShapeDtypeStruct(shape, f32)] *...  2.07 us

profile of v3, /device:TPU:8, one launch (start us, length us, event | category | flops | bytes accessed | tf_op | source)
XLA Modules:
  0.0 44.7 jit_solution(16982048231483323919)
XLA Ops:
  0.6 41.9 %thermal_creep_step.1 = (f32[2,64,16,128]{3,2,1,0:T(8,128)S(1)}, f32[2,64,16,128]{3,2,1,0:T(8,128)S(1)}, f32[2,64,16,128]{3,2,1,0:T(8,128)S(1)}, f32[2,64,16,128]{3,2,1,0:T(8,128)S(1)}) custom-call(f32[64,16,256]{2,1,0:T(8,128)} %t_in.1, f32[64,16,256]{2,1,0:T(8,128)} %src_in.1, s32[64,16,256]{2,1,0:T(8,128)} %code_in.1, s32[64,16,256]{2,1,0:T(8,128)} %flag_in.1, ...), custom_call_target="tpu_custom_call" | custom-call | tf_op jit(solution)/shard_map/thermal_creep_step/pallas_call | solution.py:600
  42.6 2.1 %write_out.1 = (f32[64,16,256]{2,1,0:T(8,128)}, f32[64,16,256]{2,1,0:T(8,128)}, f32[64,16,256]{2,1,0:T(8,128)}, f32[64,16,256]{2,1,0:T(8,128)}) custom-call(f32[2,64,16,128]{3,2,1,0:T(8,128)S(1)} %get-tuple-element.8.temp, f32[2,64,16,128]{3,2,1,0:T(8,128)S(1)} %get-tuple-element.9.cre, f32[2,64,16,128]{3,2,1,0:T(8,128)S(1)} %get-tuple-element.10.har, ...), custom_call_target="tpu_custom_call" | custom-call | tf_op jit(solution)/shard_map/write_out/pallas_call | solution.py:611

commit v4 on v3

--- a/solution.py
+++ b/solution.py
@@ -25,7 +25,8 @@
 RATE = 0.05 * 0.22313016014842982
 
 M_START, M_RZ, M_S, M_UV, M_A, M_B, M_C, M_F = 0, 3, 4, 7, 10, 19, 25, 31
-N_MSG = 36
+M_GS, M_GA = 36, 44
+N_MSG = 60
 
 
 def rcp(x):
@@ -56,8 +57,9 @@
     code, flag, temp, src, imp,
     rk, cap, ip, el, us, vs, gxm, gxp, gym, gyp, c0, base, md, ex, fl, stress,
     mid, red, planes, abuf, qbuf,
-    sx, sy, xs, ys, rz, uvx, uvy, uvxr, uvyr, bx, by, bxr, byr, qx, qy,
-    ghost, ghosty, fx, fy, fxr, fyr, zs, zm, zp, gg, dx, pc, qend,
+    sx, sy, xs, ys, rz, uvx, uvy, uvxr, uvyr, bx, by, bxr, byr, qy,
+    ghost, fx, fy, fxr, fyr, zs, zm, zp, gg, dx, pc, qend,
+    gs_out, gs, ga_out, ga, gred, ggy, dy,
     in_sem, ss, rs,
 ):
     k = lax.axis_index("stack")
@@ -74,7 +76,10 @@
         return (where.get("stack", k), where.get("plane", p), where.get("phys", f))
 
     barrier = pltpu.get_barrier_semaphore()
-    peers = [up, down, mate] + others
+    aside = [
+        [{"stack": lax.rem(k + o, ns), **side} for o in range(4)] for side in (down, up)
+    ]
+    peers = [mate] + others + aside[0] + aside[1]
     for w in peers:
         pl.semaphore_signal(barrier, inc=1, device_id=dev(w), device_id_type=MESH)
 
@@ -221,6 +226,24 @@
         send(M_S + o, planes.at[k], planes.at[k], others[o]) for o in range(3)
     ]
 
+    eight = lax.broadcasted_iota(jnp.int32, (8, W), 0)
+
+    def tile(rows_):
+        out = jnp.zeros((8, W), jnp.float32)
+        for i, r in enumerate(rows_):
+            out = jnp.where(eight == i, r, out)
+        return out
+
+    def send_rows(first, out, into):
+        return [
+            send(first + 4 * side + o, out.at[side], into.at[1 - side, k], aside[side][o])
+            for side in (0, 1) for o in range(4)
+        ]
+
+    for side, r in ((0, 0), (1, X - 1)):
+        gs_out[side] = tile([planes[k, i, h, r : r + 1, :] for i in range(3) for h in (0, 1)])
+    spread += send_rows(M_GS, gs_out, gs)
+
     def x_shifts(ref, h, l):
         return shifted(ref, h, l, -1), shifted(ref, h, l, 1)
 
@@ -228,25 +251,26 @@
         v = pltpu.roll(hy[...], lax.rem(W - l, W), axis=1)
         return jnp.broadcast_to(v[:, 0:1], (X, W))
 
-    def y_shifts(v0, v1, e0, e1):
+    def y_shifts(v0, v1, edges=None):
         r0, r1 = pltpu.roll(v0, 1, axis=1), pltpu.roll(v1, 1, axis=1)
         q0, q1 = pltpu.roll(v0, W - 1, axis=1), pltpu.roll(v1, W - 1, axis=1)
+        m1, p0 = jnp.where(lane == 0, r0, r1), jnp.where(lane == W - 1, q1, q0)
+        if edges is None:
+            return (r0, p0), (m1, q1)
         return (
-            (jnp.where(lane == 0, e0, r0), jnp.where(lane == W - 1, q1, q0)),
-            (jnp.where(lane == 0, r0, r1), jnp.where(lane == W - 1, e1, q1)),
+            (jnp.where(lane == 0, edges[0], r0), p0),
+            (m1, jnp.where(lane == W - 1, edges[1], q1)),
         )
 
-    start[2].wait_recv()
     lat = jnp.float32(LAT)
     sxm = jnp.where(row == 0, zero, lat)
     sxp = jnp.where(row == X - 1, zero, lat)
-    sym = (jnp.where((lane == 0) & first_col, zero, lat), lat)
-    syp = (lat, jnp.where((lane == W - 1) & last_col, zero, lat))
+    sym = (jnp.where(lane == 0, zero, lat), lat)
+    syp = (lat, jnp.where(lane == W - 1, zero, lat))
 
     def lateral(l, _):
-        hy = column_of(ys.at[0], l)
         kc = (rk[0, l + 1], rk[1, l + 1])
-        ysh = y_shifts(kc[0], kc[1], hy, hy)
+        ysh = y_shifts(kc[0], kc[1])
         for h in (0, 1):
             km, kp = x_shifts(rk, h, l)
             a = sxm * rcp(kc[h] + km)
@@ -270,12 +294,11 @@
         send(M_UV + 2, uvy, uvyr, mate),
     ]
 
-    def right_side(hy_ref):
+    def right_side():
         def body(l, carry):
             bf, bl = carry
-            hy = column_of(hy_ref, l)
             tc = (temp[0, l + 1], temp[1, l + 1])
-            ysh = y_shifts(tc[0], tc[1], hy, hy)
+            ysh = y_shifts(tc[0], tc[1])
             nf, nl = [], []
             for h in (0, 1):
                 tm, tp = x_shifts(temp, h, l)
@@ -295,7 +318,28 @@
         view = ref.reshape(2, ref.shape[1] * X, W)
         return view[h, pl.ds(off * X + (0 if s == 0 else X - 1), L, stride=X), :]
 
-    def ghost_terms(ghost_rows, bf, bl):
+    edge_lane = (W - 1) * (1 - f)
+    edge_masks = ((lane == 0) & last_col, (lane == W - 1) & first_col)
+
+    def add_column():
+        def body(l, _):
+            hy = column_of(dy, l)
+            rhs[1 - f, l] = rhs[1 - f, l] + jnp.where(lane == edge_lane, hy, zero)
+            return 0
+
+        loop(L, body, 0, 8)
+
+    def edge_column(q, j, shift):
+        return jnp.broadcast_to(pltpu.roll(q[j], shift, axis=1)[:, 0:1], (X, W))
+
+    def ghost_terms(ghost_rows, ghost_column, own_column, bf, bl):
+        d = jnp.where(lane < L, ggy[...] * (ghost_column - own_column), zero)
+        dy[...] = d
+        sums = [jnp.sum(uvy[j] * d, axis=1, keepdims=True) for j in (0, 1)]
+        bf, bl = [
+            [old[h] + jnp.where(edge_masks[h], sums[j], zero) for h in (0, 1)]
+            for j, old in ((0, bf), (1, bl))
+        ]
         nf, nl = [], []
         for h in (0, 1):
             f_sum, l_sum = [], []
@@ -380,37 +424,76 @@
 
         loop(L, body, 0, 4)
 
-    hy_ref = ys.at[1]
+    def interface_system(part, put):
+        a1 = part(0, 1) + part(1, 0)
+        a2 = part(1, 1) + part(2, 0)
+        a3 = part(2, 1) + part(3, 0)
+        b1, b2 = part(1, 2), part(2, 2)
+        d12 = a1 * a2 - b1 * b1
+        idet = rcp(d12 * a3 - a1 * (b2 * b2))
+        v11, v12, v13 = (a2 * a3 - b2 * b2) * idet, b1 * a3 * idet, b1 * b2 * idet
+        v22, v23, v33 = a1 * a3 * idet, a1 * b2 * idet, d12 * idet
+        table = ((v11, v12, v13), (v12, v22, v23), (v13, v23, v33))
+        for j in range(3):
+            for r, sign in ((0, 1.0), (1, -1.0)):
+                at = k + r
+                v = jnp.where(
+                    at == 1, table[0][j],
+                    jnp.where(at == 2, table[1][j], jnp.where(at == 3, table[2][j], zero)),
+                )
+                put(r, j, v * sign)
+
     loaded("src")
     for n in range(TSTEPS):
-        bf, bl = right_side(hy_ref)
+        bf, bl = right_side()
         if n == 0:
-            for m in start[:2]:
+            for m in start:
                 m.wait_recv()
             for s in (0, 1):
                 wide = jnp.where(p == (0 if s == 0 else np_ - 1), zero, lat)
                 for h in (0, 1):
                     gg[s, h] = wide * rcp(sx[s, 0, h] + xs[s, 0, h])
-            bf, bl = ghost_terms(xs.at[:, 1], bf, bl)
+            ggy[...] = jnp.where(lane < L, lat * rcp(sy[0] + ys[0]), zero)
+            bf, bl = ghost_terms(xs.at[:, 1], ys[1], sy[1], bf, bl)
         else:
-            for m in bases[:2] + fluxes[:2]:
+            if n == 1:
+                for m in uv:
+                    m.wait_recv()
+            for m in bases + beside_flux + ghost_ends:
                 m.wait_recv()
-            for side, at in ((0, 7), (1, 0)):
+            for side in (0, 1):
+                d = [ga[n - 1, side, j, 2:4, :] - ga[n - 1, side, j + 1, 0:2, :] for j in range(3)]
+                qg = [
+                    gred[side, r, 0, 0:2, :] * d[0] + gred[side, r, 1, 0:2, :] * d[1]
+                    + gred[side, r, 2, 0:2, :] * d[2]
+                    for r in (0, 1)
+                ]
                 for h in (0, 1):
                     ghost[side, h] = bxr[n - 1, side, h] + (
-                        uvxr[side, 0, h] * qx[n - 1, side, 0, h, at : at + 1, :]
-                        + uvxr[side, 1, h] * qx[n - 1, side, 1, h, at : at + 1, :]
+                        uvxr[side, 0, h] * qg[0][h : h + 1, :] + uvxr[side, 1, h] * qg[1][h : h + 1, :]
                     )
-            bf, bl = ghost_terms(ghost, bf, bl)
+            far = [edge_column(qy.at[n - 1], j, f) for j in (0, 1)]
+            near = [edge_column(qbuf.at[n - 1, :, 1 - f], j, 1 - f) for j in (0, 1)]
+            bf, bl = ghost_terms(
+                ghost,
+                byr[n - 1] + (uvyr[0] * far[0] + uvyr[1] * far[1]),
+                by[n - 1] + (uvy[0] * near[0] + uvy[1] * near[1]),
+                bf, bl,
+            )
         for h in (0, 1):
             abuf[n, k, 0, h] = bf[h]
             abuf[n, k, 1, h] = bl[h]
         ends = [
             send(M_A + 3 * n + o, abuf.at[n, k], abuf.at[n, k], others[o]) for o in range(3)
         ]
+        more = n < TSTEPS - 1
+        if more:
+            for side, r in ((0, 0), (1, X - 1)):
+                ga_out[n, side] = tile([v[h][r : r + 1, :] for v in (bf, bl) for h in (0, 1)])
+            ghost_ends = send_rows(M_GA + 8 * n, ga_out.at[n], ga.at[n])
         add_rows(rhs, dx)
+        add_column()
         block_solve()
-        more = n < TSTEPS - 1
         if more:
             for side in (0, 1):
                 pack_rows(base, bx.at[n, side], side, 0)
@@ -428,23 +511,14 @@
                 pack_column(a, 0, pc.at[2 + j])
             for m in spread:
                 m.wait_recv()
-            a1 = planes[0, 1] + planes[1, 0]
-            a2 = planes[1, 1] + planes[2, 0]
-            a3 = planes[2, 1] + planes[3, 0]
-            b1, b2 = planes[1, 2], planes[2, 2]
-            d12 = a1 * a2 - b1 * b1
-            idet = rcp(d12 * a3 - a1 * (b2 * b2))
-            v11, v12, v13 = (a2 * a3 - b2 * b2) * idet, b1 * a3 * idet, b1 * b2 * idet
-            v22, v23, v33 = a1 * a3 * idet, a1 * b2 * idet, d12 * idet
-            table = ((v11, v12, v13), (v12, v22, v23), (v13, v23, v33))
-            for j in range(3):
-                for r, shift, sign in ((0, 0, 1.0), (1, 1, -1.0)):
-                    at = k + shift
-                    v = jnp.where(
-                        at == 1, table[0][j],
-                        jnp.where(at == 2, table[1][j], jnp.where(at == 3, table[2][j], zero)),
-                    )
-                    red[r, j] = v * sign
+            interface_system(
+                lambda j, i: planes[j, i], lambda r, j, v: red.__setitem__((r, j), v)
+            )
+            for side in (0, 1):
+                interface_system(
+                    lambda j, i, side=side: gs[side, j, 2 * i : 2 * i + 2, :],
+                    lambda r, j, v, side=side: gred.__setitem__((side, r, j, slice(0, 2)), v),
+                )
         else:
             if n == 1:
                 for name in ("cre", "har"):
@@ -462,32 +536,11 @@
         ]
         if more:
             qbuf[n, 0], qbuf[n, 1] = qt, qb
-            fluxes = [
-                send(M_C + 3 * n, qbuf.at[n, :, :, pl.ds(8, 8)], qx.at[n, 0], up),
-                send(M_C + 3 * n + 1, qbuf.at[n, :, :, pl.ds(0, 8)], qx.at[n, 1], down),
-                send(M_C + 3 * n + 2, qbuf.at[n, :, 1 - f], qy.at[n], mate),
-            ]
+            beside_flux = [send(M_C + 3 * n + 2, qbuf.at[n, :, 1 - f], qy.at[n], mate)]
         if more:
             correct(qt, qb)
-            if n == 0:
-                for m in uv:
-                    m.wait_recv()
-            bases[2].wait_recv()
-            fluxes[2].wait_recv()
-            col = [
-                jnp.broadcast_to(pltpu.roll(qy[n, s], f, axis=1)[:, 0:1], (X, W)) for s in (0, 1)
-            ]
-            ghosty[...] = byr[n] + (uvyr[0] * col[0] + uvyr[1] * col[1])
-            hy_ref = ghosty
 
     qend[0], qend[1] = qt, qb
-    col = [
-        jnp.broadcast_to(pltpu.roll(qend[j, 1 - f], 1 - f, axis=1)[:, 0:1], (X, W)) for j in (0, 1)
-    ]
-    tc = pc[6] + (uvy[0] * col[0] + uvy[1] * col[1])
-    used = jnp.where(lane < L, pc[1], jnp.float32(1.0))
-    fy[...] = creep_cell(tc, pc[0], used, *[pc[2 + j] for j in range(4)])[2]
-    beside = send(M_F + 2, fy, fyr, mate)
     for s, r in ((0, 0), (1, X - 1)):
         for h in (0, 1):
             t = side_row(base, s, h, 0) + (
@@ -502,8 +555,15 @@
         send(M_F + 3, zs.at[1], zm, others[0]),
         send(M_F + 4, zs.at[0], zp, others[2]),
     ]
-
-    lag = 8
+    col = [
+        jnp.broadcast_to(pltpu.roll(qend[j, 1 - f], 1 - f, axis=1)[:, 0:1], (X, W)) for j in (0, 1)
+    ]
+    tc = pc[6] + (uvy[0] * col[0] + uvy[1] * col[1])
+    used = jnp.where(lane < L, pc[1], jnp.float32(1.0))
+    fy[...] = creep_cell(tc, pc[0], used, *[pc[2 + j] for j in range(4)])[2]
+    beside = send(M_F + 2, fy, fyr, mate)
+
+    lag = 16
 
     def last_creep(i):
         t = solved(i, qt, qb)
@@ -514,7 +574,7 @@
         hy = column_of(fyr, l)
         sc = (stress[0, l + 1], stress[1, l + 1])
         ysh = y_shifts(
-            sc[0], sc[1], jnp.where(first_col, zero, hy), jnp.where(last_col, zero, hy)
+            sc[0], sc[1], (jnp.where(first_col, zero, hy), jnp.where(last_col, zero, hy))
         )
         for h in (0, 1):
             sm, sp = x_shifts(stress, h, l)
@@ -587,12 +647,14 @@
         vm(2, X, W),
         vm(2, 2, 2, L, W), vm(2, X, W), vm(2, 2, 2, L, W), vm(2, X, W),
         vm(2, 2, 2, L, W), vm(2, X, W), vm(2, 2, 2, L, W), vm(2, X, W),
-        vm(2, 2, 2, 2, 8, W), vm(2, 2, X, W),
-        vm(2, 2, L, W), vm(X, W),
+        vm(2, 2, X, W),
+        vm(2, 2, L, W),
         vm(2, 2, L, W), vm(X, W), vm(2, 2, L, W), vm(X, W),
         vm(2, 2, X, W), vm(2, X, W), vm(2, X, W),
         vm(2, 2, L, W), vm(2, 2, L, W),
         vm(7, X, W), vm(2, 2, X, W),
+        vm(2, 8, W), vm(2, 4, 8, W), vm(2, 2, 8, W), vm(2, 2, 4, 8, W),
+        vm(2, 2, 3, 8, W), vm(X, W), vm(X, W),
         pltpu.SemaphoreType.DMA((7, 2)),
         pltpu.SemaphoreType.DMA((N_MSG,)), pltpu.SemaphoreType.DMA((N_MSG,)),
     ]

time: 45.6 us -> 44.6 us (0.978); the launches traced: 44.7 us -> 44.2 us
  no operation moved by 1% of the time
where the time goes in v4:
time: 44.6 us; the launch traced here: 44.2 us
  Pallas kernels  43.6 us (98%)
  between operations  0.64 us (1%)
    pallas_call x1, Pallas kernels, per_device(): pl.pallas_call(kernel, out_shape=[jax.ShapeDtypeStruct(s, f32) for s in (...  41.5 us
    pallas_call x1, Pallas kernels, per_device(): pl.pallas_call(write_out, out_shape=[jax.ShapeDtypeStruct(shape, f32)] *...  2.07 us

profile of v4, /device:TPU:8, one launch (start us, length us, event | category | flops | bytes accessed | tf_op | source)
XLA Modules:
  0.0 44.2 jit_solution(14357565297932207839)
XLA Ops:
  0.6 41.5 %thermal_creep_step.1 = (f32[2,64,16,128]{3,2,1,0:T(8,128)S(1)}, f32[2,64,16,128]{3,2,1,0:T(8,128)S(1)}, f32[2,64,16,128]{3,2,1,0:T(8,128)S(1)}, f32[2,64,16,128]{3,2,1,0:T(8,128)S(1)}) custom-call(f32[64,16,256]{2,1,0:T(8,128)} %t_in.1, f32[64,16,256]{2,1,0:T(8,128)} %src_in.1, s32[64,16,256]{2,1,0:T(8,128)} %code_in.1, s32[64,16,256]{2,1,0:T(8,128)} %flag_in.1, ...), custom_call_target="tpu_custom_call" | custom-call | tf_op jit(solution)/shard_map/thermal_creep_step/pallas_call | solution.py:662
  42.1 2.1 %write_out.1 = (f32[64,16,256]{2,1,0:T(8,128)}, f32[64,16,256]{2,1,0:T(8,128)}, f32[64,16,256]{2,1,0:T(8,128)}, f32[64,16,256]{2,1,0:T(8,128)}) custom-call(f32[2,64,16,128]{3,2,1,0:T(8,128)S(1)} %get-tuple-element.8.temp, f32[2,64,16,128]{3,2,1,0:T(8,128)S(1)} %get-tuple-element.9.cre, f32[2,64,16,128]{3,2,1,0:T(8,128)S(1)} %get-tuple-element.10.har, ...), custom_call_target="tpu_custom_call" | custom-call | tf_op jit(solution)/shard_map/write_out/pallas_call | solution.py:673

commit v5 on v4

--- a/solution.py
+++ b/solution.py
@@ -148,12 +148,17 @@
         for h in (0, 1):
             dst[h] = view[h, pl.ds(off * X + r, L, stride=X), :]
 
-    def pack_column(ref, off, dst):
+    def pack_columns(*items):
         def body(l, acc):
-            v = pltpu.roll(ref[1 - f, l + off], lax.rem(l + 1 - f, W), axis=1)
-            return jnp.where(lane == l, v, acc)
-
-        dst[...] = loop(L, body, jnp.zeros((X, W), jnp.float32), L)
+            shift = lax.rem(l + 1 - f, W)
+            return tuple(
+                jnp.where(lane == l, pltpu.roll(ref[1 - f, l + off], shift, axis=1), old)
+                for old, (ref, off, _) in zip(acc, items)
+            )
+
+        z = jnp.zeros((X, W), jnp.float32)
+        for value, (_, _, dst) in zip(loop(L, body, (z,) * len(items), L), items):
+            dst[...] = value
 
     loaded("temp")
     load("flag", "imp", "cre", "har")
@@ -166,9 +171,44 @@
         send(M_START + 1, sx.at[0], xs.at[1], down),
     ]
     to_below = send(M_RZ, rk.at[:, L], rz, others[0])
-    pack_column(rk, 1, sy.at[0])
-    pack_column(temp, 1, sy.at[1])
+    pack_columns((rk, 1, sy.at[0]), (temp, 1, sy.at[1]))
     start.append(send(M_START + 2, sy, ys, mate))
+
+    def x_shifts(ref, h, l):
+        return shifted(ref, h, l, -1), shifted(ref, h, l, 1)
+
+    def column_of(hy, l):
+        v = pltpu.roll(hy[...], lax.rem(W - l, W), axis=1)
+        return jnp.broadcast_to(v[:, 0:1], (X, W))
+
+    def y_shifts(v0, v1, edges=None):
+        r0, r1 = pltpu.roll(v0, 1, axis=1), pltpu.roll(v1, 1, axis=1)
+        q0, q1 = pltpu.roll(v0, W - 1, axis=1), pltpu.roll(v1, W - 1, axis=1)
+        m1, p0 = jnp.where(lane == 0, r0, r1), jnp.where(lane == W - 1, q1, q0)
+        if edges is None:
+            return (r0, p0), (m1, q1)
+        return (
+            (jnp.where(lane == 0, edges[0], r0), p0),
+            (m1, jnp.where(lane == W - 1, edges[1], q1)),
+        )
+
+    lat = jnp.float32(LAT)
+    sxm = jnp.where(row == 0, zero, lat)
+    sxp = jnp.where(row == X - 1, zero, lat)
+    sym = (jnp.where(lane == 0, zero, lat), lat)
+    syp = (lat, jnp.where(lane == W - 1, zero, lat))
+
+    def lateral(l):
+        kc = (rk[0, l + 1], rk[1, l + 1])
+        ysh = y_shifts(kc[0], kc[1])
+        for h in (0, 1):
+            km, kp = x_shifts(rk, h, l)
+            a = sxm * rcp(kc[h] + km)
+            b = sxp * rcp(kc[h] + kp)
+            c = sym[h] * rcp(kc[h] + ysh[h][0])
+            d = syp[h] * rcp(kc[h] + ysh[h][1])
+            gxm[h, l], gxp[h, l], gym[h, l], gyp[h, l] = a, b, c, d
+            c0[h, l] = cap[h, l] - ((a + b) + (c + d))
 
     one = jnp.ones((2, X, W), jnp.float32)
     top_cap = cap[:, 0] + jnp.where(k == 0, jnp.float32(H_CONV), zero)
@@ -193,6 +233,8 @@
         ip[:, m] = ipb
         el[:, m] = eb
         vs[:, m] = ipb * wb
+        lateral(i)
+        lateral(m)
         return dn, nn, e * wt, dbn, nbn, eb * wb
 
     dt, nt, wt, db, nb, wb = loop(
@@ -217,7 +259,9 @@
         us[:, l], vs[:, l], us[:, m], vs[:, m] = ut, vt, ub, vb
         return ut, ub, vt, vb
 
-    ut, ub, vt, vb = loop(HALF - 1, spikes, (ut, ub, vt, vb), 4)
+    lateral(HALF - 1)
+    lateral(HALF)
+    ut, ub, vt, vb = loop(HALF - 1, spikes, (ut, ub, vt, vb), 8)
     to_below.wait_recv()
     planes[k, 0] = ut + rz[...] + rk[:, 1]
     planes[k, 1] = vb
@@ -244,50 +288,10 @@
         gs_out[side] = tile([planes[k, i, h, r : r + 1, :] for i in range(3) for h in (0, 1)])
     spread += send_rows(M_GS, gs_out, gs)
 
-    def x_shifts(ref, h, l):
-        return shifted(ref, h, l, -1), shifted(ref, h, l, 1)
-
-    def column_of(hy, l):
-        v = pltpu.roll(hy[...], lax.rem(W - l, W), axis=1)
-        return jnp.broadcast_to(v[:, 0:1], (X, W))
-
-    def y_shifts(v0, v1, edges=None):
-        r0, r1 = pltpu.roll(v0, 1, axis=1), pltpu.roll(v1, 1, axis=1)
-        q0, q1 = pltpu.roll(v0, W - 1, axis=1), pltpu.roll(v1, W - 1, axis=1)
-        m1, p0 = jnp.where(lane == 0, r0, r1), jnp.where(lane == W - 1, q1, q0)
-        if edges is None:
-            return (r0, p0), (m1, q1)
-        return (
-            (jnp.where(lane == 0, edges[0], r0), p0),
-            (m1, jnp.where(lane == W - 1, edges[1], q1)),
-        )
-
-    lat = jnp.float32(LAT)
-    sxm = jnp.where(row == 0, zero, lat)
-    sxp = jnp.where(row == X - 1, zero, lat)
-    sym = (jnp.where(lane == 0, zero, lat), lat)
-    syp = (lat, jnp.where(lane == W - 1, zero, lat))
-
-    def lateral(l, _):
-        kc = (rk[0, l + 1], rk[1, l + 1])
-        ysh = y_shifts(kc[0], kc[1])
-        for h in (0, 1):
-            km, kp = x_shifts(rk, h, l)
-            a = sxm * rcp(kc[h] + km)
-            b = sxp * rcp(kc[h] + kp)
-            c = sym[h] * rcp(kc[h] + ysh[h][0])
-            d = syp[h] * rcp(kc[h] + ysh[h][1])
-            gxm[h, l], gxp[h, l], gym[h, l], gyp[h, l] = a, b, c, d
-            c0[h, l] = cap[h, l] - ((a + b) + (c + d))
-        return 0
-
-    loop(L, lateral, 0, 8)
-
     for side in (0, 1):
         pack_rows(us, uvx.at[side, 0], side, 0)
         pack_rows(vs, uvx.at[side, 1], side, 0)
-    pack_column(us, 0, uvy.at[0])
-    pack_column(vs, 0, uvy.at[1])
+    pack_columns((us, 0, uvy.at[0]), (vs, 0, uvy.at[1]))
     uv = [
         send(M_UV, uvx.at[1], uvxr.at[0], up),
         send(M_UV + 1, uvx.at[0], uvxr.at[1], down),
@@ -312,7 +316,7 @@
             return tuple(nf), tuple(nl)
 
         z = jnp.zeros((X, W), jnp.float32)
-        return loop(L, body, ((z, z), (z, z)), 8)
+        return loop(L, body, ((z, z), (z, z)), 16)
 
     def side_row(ref, s, h, off):
         view = ref.reshape(2, ref.shape[1] * X, W)
@@ -497,7 +501,7 @@
         if more:
             for side in (0, 1):
                 pack_rows(base, bx.at[n, side], side, 0)
-            pack_column(base, 0, by.at[n])
+            pack_columns((base, 0, by.at[n]))
             bases = [
                 send(M_B + 3 * n, bx.at[n, 1], bxr.at[n, 0], up),
                 send(M_B + 3 * n + 1, bx.at[n, 0], bxr.at[n, 1], down),
@@ -507,8 +511,8 @@
             loaded("flag")
             loop(L // 2, creep_tables, 0, 2)
             loaded("imp")
-            for j, a in enumerate((md, ex, imp, fl)):
-                pack_column(a, 0, pc.at[2 + j])
+            pack_columns((md, 0, pc.at[2]), (ex, 0, pc.at[3]))
+            pack_columns((imp, 0, pc.at[4]), (fl, 0, pc.at[5]))
             for m in spread:
                 m.wait_recv()
             interface_system(
@@ -525,9 +529,7 @@
                     loaded(name)
             creep()
             if not more:
-                pack_column(base, 0, pc.at[6])
-                pack_column(cre, 0, pc.at[0])
-                pack_column(har, 0, pc.at[1])
+                pack_columns((base, 0, pc.at[6]), (cre, 0, pc.at[0]), (har, 0, pc.at[1]))
         for m in ends:
             m.wait_recv()
         r = [abuf[n, j, 1] - abuf[n, j + 1, 0] for j in range(3)]
@@ -599,7 +601,7 @@
 
     loop(lag, first_layers, 0, 4)
     beside.wait_recv()
-    loop(L - lag, both, 0, 4)
+    loop(L - lag, both, 0, 6)
     loop(lag, last_layers, 0, 8)
     for m in edges:
         m.wait_recv()

time: 44.6 us -> 44.6 us (level)
  no operation moved by 1% of the time
where the time goes in v5:
time: 44.6 us; the launch traced here: 44.5 us
  Pallas kernels  43.8 us (98%)
  between operations  0.64 us (1%)
    pallas_call x1, Pallas kernels, per_device(): pl.pallas_call(kernel, out_shape=[jax.ShapeDtypeStruct(s, f32) for s in (...  41.7 us
    pallas_call x1, Pallas kernels, per_device(): pl.pallas_call(write_out, out_shape=[jax.ShapeDtypeStruct(shape, f32)] *...  2.07 us

profile of v5, /device:TPU:8, one launch (start us, length us, event | category | flops | bytes accessed | tf_op | source)
XLA Modules:
  0.0 44.5 jit_solution(14462266029552435526)
XLA Ops:
  0.6 41.7 %thermal_creep_step.1 = (f32[2,64,16,128]{3,2,1,0:T(8,128)S(1)}, f32[2,64,16,128]{3,2,1,0:T(8,128)S(1)}, f32[2,64,16,128]{3,2,1,0:T(8,128)S(1)}, f32[2,64,16,128]{3,2,1,0:T(8,128)S(1)}) custom-call(f32[64,16,256]{2,1,0:T(8,128)} %t_in.1, f32[64,16,256]{2,1,0:T(8,128)} %src_in.1, s32[64,16,256]{2,1,0:T(8,128)} %code_in.1, s32[64,16,256]{2,1,0:T(8,128)} %flag_in.1, ...), custom_call_target="tpu_custom_call" | custom-call | tf_op jit(solution)/shard_map/thermal_creep_step/pallas_call | solution.py:664
  42.4 2.1 %write_out.1 = (f32[64,16,256]{2,1,0:T(8,128)}, f32[64,16,256]{2,1,0:T(8,128)}, f32[64,16,256]{2,1,0:T(8,128)}, f32[64,16,256]{2,1,0:T(8,128)}) custom-call(f32[2,64,16,128]{3,2,1,0:T(8,128)S(1)} %get-tuple-element.8.temp, f32[2,64,16,128]{3,2,1,0:T(8,128)S(1)} %get-tuple-element.9.cre, f32[2,64,16,128]{3,2,1,0:T(8,128)S(1)} %get-tuple-element.10.har, ...), custom_call_target="tpu_custom_call" | custom-call | tf_op jit(solution)/shard_map/write_out/pallas_call | solution.py:675

commit v6 on v5

--- a/solution.py
+++ b/solution.py
@@ -316,7 +316,7 @@
             return tuple(nf), tuple(nl)
 
         z = jnp.zeros((X, W), jnp.float32)
-        return loop(L, body, ((z, z), (z, z)), 16)
+        return loop(L, body, ((z, z), (z, z)), 32)
 
     def side_row(ref, s, h, off):
         view = ref.reshape(2, ref.shape[1] * X, W)
@@ -488,7 +488,7 @@
             abuf[n, k, 0, h] = bf[h]
             abuf[n, k, 1, h] = bl[h]
         ends = [
-            send(M_A + 3 * n + o, abuf.at[n, k], abuf.at[n, k], others[o]) for o in range(3)
+            send(M_A + 3 * n + o, abuf.at[n, k], abuf.at[n, k], others[o]) for o in (1, 0, 2)
         ]
         more = n < TSTEPS - 1
         if more:

time: 44.6 us -> 44.6 us (level)
  no operation moved by 1% of the time
where the time goes in v6:
time: 44.6 us; the launch traced here: 44.5 us
  Pallas kernels  43.8 us (98%)
  between operations  0.64 us (1%)
    pallas_call x1, Pallas kernels, per_device(): pl.pallas_call(kernel, out_shape=[jax.ShapeDtypeStruct(s, f32) for s in (...  41.7 us
    pallas_call x1, Pallas kernels, per_device(): pl.pallas_call(write_out, out_shape=[jax.ShapeDtypeStruct(shape, f32)] *...  2.07 us

profile of v6, /device:TPU:8, one launch (start us, length us, event | category | flops | bytes accessed | tf_op | source)
XLA Modules:
  0.0 44.5 jit_solution(10651881075753503831)
XLA Ops:
  0.6 41.7 %thermal_creep_step.1 = (f32[2,64,16,128]{3,2,1,0:T(8,128)S(1)}, f32[2,64,16,128]{3,2,1,0:T(8,128)S(1)}, f32[2,64,16,128]{3,2,1,0:T(8,128)S(1)}, f32[2,64,16,128]{3,2,1,0:T(8,128)S(1)}) custom-call(f32[64,16,256]{2,1,0:T(8,128)} %t_in.1, f32[64,16,256]{2,1,0:T(8,128)} %src_in.1, s32[64,16,256]{2,1,0:T(8,128)} %code_in.1, s32[64,16,256]{2,1,0:T(8,128)} %flag_in.1, ...), custom_call_target="tpu_custom_call" | custom-call | tf_op jit(solution)/shard_map/thermal_creep_step/pallas_call | solution.py:664
  42.4 2.1 %write_out.1 = (f32[64,16,256]{2,1,0:T(8,128)}, f32[64,16,256]{2,1,0:T(8,128)}, f32[64,16,256]{2,1,0:T(8,128)}, f32[64,16,256]{2,1,0:T(8,128)}) custom-call(f32[2,64,16,128]{3,2,1,0:T(8,128)S(1)} %get-tuple-element.8.temp, f32[2,64,16,128]{3,2,1,0:T(8,128)S(1)} %get-tuple-element.9.cre, f32[2,64,16,128]{3,2,1,0:T(8,128)S(1)} %get-tuple-element.10.har, ...), custom_call_target="tpu_custom_call" | custom-call | tf_op jit(solution)/shard_map/write_out/pallas_call | solution.py:675

commit v7 on v5

--- a/solution.py
+++ b/solution.py
@@ -565,7 +565,7 @@
     fy[...] = creep_cell(tc, pc[0], used, *[pc[2 + j] for j in range(4)])[2]
     beside = send(M_F + 2, fy, fyr, mate)
 
-    lag = 16
+    lag = 24
 
     def last_creep(i):
         t = solved(i, qt, qb)

time: 44.6 us -> 44.6 us (level)
  no operation moved by 1% of the time
where the time goes in v7:
time: 44.6 us; the launch traced here: 44.5 us
  Pallas kernels  43.8 us (98%)
  between operations  0.64 us (1%)
    pallas_call x1, Pallas kernels, per_device(): pl.pallas_call(kernel, out_shape=[jax.ShapeDtypeStruct(s, f32) for s in (...  41.7 us
    pallas_call x1, Pallas kernels, per_device(): pl.pallas_call(write_out, out_shape=[jax.ShapeDtypeStruct(shape, f32)] *...  2.07 us

profile of v7, /device:TPU:8, one launch (start us, length us, event | category | flops | bytes accessed | tf_op | source)
XLA Modules:
  0.0 44.5 jit_solution(12670149272982910718)
XLA Ops:
  0.6 41.7 %thermal_creep_step.1 = (f32[2,64,16,128]{3,2,1,0:T(8,128)S(1)}, f32[2,64,16,128]{3,2,1,0:T(8,128)S(1)}, f32[2,64,16,128]{3,2,1,0:T(8,128)S(1)}, f32[2,64,16,128]{3,2,1,0:T(8,128)S(1)}) custom-call(f32[64,16,256]{2,1,0:T(8,128)} %t_in.1, f32[64,16,256]{2,1,0:T(8,128)} %src_in.1, s32[64,16,256]{2,1,0:T(8,128)} %code_in.1, s32[64,16,256]{2,1,0:T(8,128)} %flag_in.1, ...), custom_call_target="tpu_custom_call" | custom-call | tf_op jit(solution)/shard_map/thermal_creep_step/pallas_call | solution.py:664
  42.4 2.1 %write_out.1 = (f32[64,16,256]{2,1,0:T(8,128)}, f32[64,16,256]{2,1,0:T(8,128)}, f32[64,16,256]{2,1,0:T(8,128)}, f32[64,16,256]{2,1,0:T(8,128)}) custom-call(f32[2,64,16,128]{3,2,1,0:T(8,128)S(1)} %get-tuple-element.8.temp, f32[2,64,16,128]{3,2,1,0:T(8,128)S(1)} %get-tuple-element.9.cre, f32[2,64,16,128]{3,2,1,0:T(8,128)S(1)} %get-tuple-element.10.har, ...), custom_call_target="tpu_custom_call" | custom-call | tf_op jit(solution)/shard_map/write_out/pallas_call | solution.py:675
